TPU v7x, 32 devices: a whole 2x2x4 slice. The times are simulated.
32 devices in a mesh: inst: 4 (over x, core), space: 8 (over z, y).
Axes of the slice: x: 2, y: 2, z: 4, core: 2. Of those that a mesh axis runs over, the one named last changes fastest.
Arguments:
- adjoint_old: float32 [8, 6, 512, 512], P('inst', None, 'space'), may hold values from -6 to 6
- source_term: float32 [8, 6, 512, 512], P('inst', None, 'space'), may hold values from -6 to 6
- face_stream: float32 [8, 512, 512], P('inst', 'space'), may hold values from 0.2 to 1
- face_pitch: float32 [8, 512, 512], P('inst', 'space'), may hold values from 0.2 to 1
- diag_scale: float32 [8, 512, 512], P('inst', 'space'), may hold values from 0.1 to 0.4
- volume: float32 [512, 512], P('space'), may hold values from 0.5 to 2
- face_blocks: float32 [4, 6, 6], replicated, may hold values from -2.5 to 2.5
- diag_inverse: float32 [8, 6, 6], P('inst')
- periodic_block: float32 [6, 6], replicated, may hold values from -2.5 to 2.5
- frequency: float32 [1], replicated, may hold values from 0.5 to 2
- phase_shift: int32 [1], replicated, may hold values from 1 to 7
- periodic_cells: int32 [8, 8, 128], P('space'), may hold values from 0 to 32767
- periodic_targets: int32 [8, 8, 128], P(None, 'space'), may hold values from 0 to 32767
- periodic_weights: float32 [8, 8, 128], P('space'), may hold values from 0.5 to 1.5
- periodic_counts: int32 [8, 8], P('space'), may hold values from 0 to 128, as said below
Outputs:
- adjoint_new: float32 [8, 6, 512, 512], P('inst', None, 'space')
- residual: float32 [8, 6, 512, 512], P('inst', None, 'space')
Inputs may be any that keep to these rules, and one draw needn't show every extreme that they name: `periodic_counts`: each partition's row has one peer with 128 live faces, and one partition receives 128 live faces from every partition. `periodic_cells`: local cell indices in the sending partition. `periodic_targets`: local cell indices in the receiving partition.
All inputs are finite; a program needn't handle non-finite values.
Results may differ from a plain program's by a relative error of at most 0.0001.
Values sent between devices are 32-bit elements; how exact they have to be, the bound alone decides.
A program may use at most 128 MiB of HBM per device.

v0:
```python
import functools
import math

import jax
import jax.numpy as jnp
from jax import lax
from jax.experimental import pallas as pl
from jax.experimental.pallas import tpu as pltpu
from jax.sharding import PartitionSpec as P

SWEEPS = 2
TILE = 8
LANES = 128
WINDOW = 3
PARTS = 2
MESH = pl.DeviceIdType.MESH


def spectral_entry(offset, count):
    offset = offset % count
    if offset == 0 or 2 * offset == count:
        return 0.0
    return 0.5 * (-1.0) ** offset / math.tan(math.pi * offset / count)


def split_parts(value):
    parts = []
    for _ in range(PARTS):
        part = value.astype(jnp.bfloat16)
        parts.append(part)
        value = value - part.astype(jnp.float32)
    return parts


def kernel(
    n_space,
    a_hbm,
    s_hbm,
    fs_hbm,
    fp_hbm,
    ds_hbm,
    vol_hbm,
    blocks,
    dinv,
    pblock,
    freq,
    shift,
    cells,
    targets,
    weights,
    counts,
    out_a,
    out_r,
    A,
    SP,
    R,
    FS,
    FP,
    DS,
    VOL,
    RX,
    SB,
    RL,
    COL,
    PICK,
    ALLP,
    ROUTED,
    ARR,
    LHS,
    load_sem,
    xs,
    xr,
    rs,
    rr,
    ss,
    sr,
    hs,
    hr,
    ps,
    pr,
    as_,
    ar,
    oa,
    orr,
):
    per_dev, variables, rows, width = a_hbm.shape
    instances = 4 * per_dev
    slots = cells.shape[2]
    nb = rows // TILE
    total = SWEEPS * nb
    inst = lax.axis_index("inst")
    me = lax.axis_index("space")
    odd = inst % 2
    sibling = inst + 1 - 2 * odd
    across = (inst + 2) % 4
    shift_bits = width.bit_length() - 1

    def local(src, dst, n):
        return pltpu.make_async_copy(src, dst, load_sem.at[n])

    inner = pl.ds(TILE, rows)
    loads = [
        local(a_hbm, A.at[0, :, :, inner, :], 0),
        local(fs_hbm, FS.at[:, inner, :], 1),
        local(s_hbm, SP, 2),
        local(fp_hbm, FP, 3),
        local(ds_hbm, DS, 4),
        local(vol_hbm, VOL, 5),
    ]
    for copy in loads:
        copy.start()

    barrier = pltpu.get_barrier_semaphore()
    pl.semaphore_signal(barrier, inc=1, device_id={"inst": sibling}, device_id_type=MESH)
    pl.semaphore_signal(barrier, inc=1, device_id={"inst": across}, device_id_type=MESH)

    @pl.loop(1, n_space)
    def _(j):
        pl.semaphore_signal(
            barrier, inc=1, device_id={"space": (me + j) % n_space}, device_id_type=MESH
        )

    def remote(src, dst, send, recv, **device):
        return pltpu.make_async_remote_copy(
            src_ref=src, dst_ref=dst, send_sem=send, recv_sem=recv, device_id=device,
            device_id_type=MESH,
        )

    def place(t):
        sweep = t // nb
        block = (t % nb + nb - 1) % nb
        return sweep, block, pl.multiple_of(block * TILE, TILE)

    def x_copy(t):
        sweep, _, row = place(t)
        return remote(
            A.at[sweep, :, :, pl.ds(row + TILE, TILE), :],
            RX.at[sweep, :, :, pl.ds(row, TILE), :],
            xs.at[t], xr.at[t], inst=across,
        )

    def sib_copy(t):
        sweep, _, row = place(t)
        return remote(
            A.at[sweep, :, :, pl.ds(row + TILE, TILE), :],
            SB.at[sweep, :, :, pl.ds(row, TILE), :],
            ss.at[t], sr.at[t], inst=sibling,
        )

    def relay_copy(t):
        sweep, _, row = place(t)
        here = RX.at[sweep, :, :, pl.ds(row, TILE), :]
        return remote(
            here, RL.at[sweep, :, :, pl.ds(row, TILE), :], rs.at[t], rr.at[t], inst=sibling
        )

    def forward(t):
        x_copy(t).wait()
        relay_copy(t).start()

    has_above = me < n_space - 1
    has_below = me > 0
    above = (me + 1) % n_space
    below = (me + n_space - 1) % n_space

    def halo_up(sweep):
        return remote(
            A.at[sweep, :, :, pl.ds(rows, TILE), :],
            A.at[sweep, :, :, pl.ds(0, TILE), :],
            hs.at[2 * sweep], hr.at[2 * sweep], space=above,
        )

    def halo_down(sweep):
        return remote(
            A.at[sweep, :, :, pl.ds(TILE, TILE), :],
            A.at[sweep, :, :, pl.ds(rows + TILE, TILE), :],
            hs.at[2 * sweep + 1], hr.at[2 * sweep + 1], space=below,
        )

    def halo_face():
        last = 2 * SWEEPS
        return remote(
            FS.at[:, pl.ds(rows, TILE), :], FS.at[:, pl.ds(0, TILE), :],
            hs.at[last], hr.at[last], space=above,
        )

    @pl.when(me == 0)
    def _():
        FS[:, 0:TILE, :] = jnp.zeros((per_dev, TILE, width), jnp.float32)
        for sweep in range(SWEEPS):
            A[sweep, :, :, 0:TILE, :] = jnp.zeros((per_dev, variables, TILE, width), jnp.float32)

    @pl.when(me == n_space - 1)
    def _():
        for sweep in range(SWEEPS):
            A[sweep, :, :, rows + TILE : rows + 2 * TILE, :] = jnp.zeros(
                (per_dev, variables, TILE, width), jnp.float32
            )

    loads[0].wait()
    pl.semaphore_wait(barrier, n_space + 1)

    @pl.loop(0, nb)
    def _(t):
        x_copy(t).start()

    loads[1].wait()

    @pl.when(has_above)
    def _():
        halo_up(0).start()
        halo_face().start()

    @pl.when(has_below)
    def _():
        halo_down(0).start()

    @pl.loop(0, nb)
    def _(t):
        sib_copy(t).start()

    sub_w = lax.broadcasted_iota(jnp.int32, (width, slots), 0)
    sub_r = lax.broadcasted_iota(jnp.int32, (rows, slots), 0)

    def column_table(index, chunk):
        for q in range(TILE):
            line = index(chunk * TILE + q)
            column = jnp.bitwise_and(line, width - 1)
            hot = jnp.where(sub_w == column, 1.0, 0.0).astype(jnp.bfloat16)
            COL[:, q * slots : (q + 1) * slots] = hot

    def cell_line(q):
        return cells[0, pl.ds(q, 1), :]

    def target_line(p):
        return targets[p, 0:1, :]

    chunks = n_space // TILE

    @pl.loop(0, chunks)
    def _(chunk):
        column_table(cell_line, chunk)

        @pl.loop(0, per_dev)
        def _(k):
            field = A[0, k, :, TILE : TILE + rows, :].reshape(variables * rows, width)
            stacked = jnp.concatenate(split_parts(field), axis=0)
            terms = jnp.dot(stacked, COL[...], preferred_element_type=jnp.float32)
            height = variables * rows
            found = terms[:height]
            for part in range(1, PARTS):
                found = found + terms[part * height : (part + 1) * height]
            for q in range(TILE):
                hit = sub_r == lax.shift_right_logical(cell_line(chunk * TILE + q), shift_bits)
                for v in range(variables):
                    piece = found[v * rows : (v + 1) * rows, q * slots : (q + 1) * slots]
                    PICK[k, v, chunk, q : q + 1, :] = jnp.sum(
                        jnp.where(hit, piece, 0.0), axis=0, keepdims=True
                    )

        lane = lax.broadcasted_iota(jnp.int32, (TILE, slots), 1)
        sub = lax.broadcasted_iota(jnp.int32, (TILE, slots), 0)
        limit = jnp.zeros((TILE, slots), jnp.int32)
        for q in range(TILE):
            limit = jnp.where(sub == q, counts[0, chunk * TILE + q], limit)
        first = pl.multiple_of(chunk * TILE, TILE)
        weight = jnp.where(lane < limit, weights[0, pl.ds(first, TILE), :], 0.0)

        for k in range(per_dev):
            picked = [PICK[k, v, chunk] for v in range(variables)]
            for u in range(variables):
                mixed = pblock[0, u] * picked[0]
                for v in range(1, variables):
                    mixed = mixed + pblock[v, u] * picked[v]
                ALLP[0, k, u, chunk] = mixed * weight

    p_x = remote(ALLP.at[0], ALLP.at[2], ps.at[0], pr.at[0], inst=across)
    p_sib = remote(ALLP.at[0], ALLP.at[3 - 2 * odd], ps.at[1], pr.at[1 + odd], inst=sibling)
    p_rel = remote(ALLP.at[2], ALLP.at[1 + 2 * odd], ps.at[2], pr.at[2 - odd], inst=sibling)
    p_sib_in = remote(ALLP.at[0], ALLP.at[1 + 2 * odd], ps.at[1], pr.at[2 - odd], inst=sibling)
    p_rel_in = remote(ALLP.at[2], ALLP.at[3 - 2 * odd], ps.at[2], pr.at[1 + odd], inst=sibling)
    p_x.start()
    p_sib.start()
    forward(0)
    p_x.wait_recv()
    p_rel.start()
    p_sib_in.wait_recv()
    p_rel_in.wait_recv()
    for k in range(per_dev):
        wanted = lax.rem(k - shift[0] + 2 * instances, instances)
        group = lax.div(wanted, per_dev)
        member = lax.rem(wanted, per_dev)

        @pl.loop(0, chunks)
        def _(chunk):
            for u in range(variables):
                value = ALLP[group, member, u, chunk]
                for q in range(TILE):
                    ROUTED[chunk * TILE + q, k, u : u + 1, :] = value[q : q + 1, :]

    def a2a(j):
        return remote(
            ROUTED.at[(me + j) % n_space], ARR.at[me], as_.at[j], ar.at[j],
            space=(me + j) % n_space,
        )

    @pl.loop(1, n_space)
    def _(j):
        a2a(j).start()

    ARR[me] = ROUTED[me]
    forward(1)
    loads[2].wait()
    column_table(target_line, 0)

    @pl.loop(1, n_space)
    def _(j):
        remote(
            ROUTED.at[0], ARR.at[(me + n_space - j) % n_space], as_.at[j], ar.at[j],
            space=(me + j) % n_space,
        ).wait_recv()

    @pl.loop(0, chunks)
    def _(chunk):
        if chunks > 1:
            column_table(target_line, chunk)

        for k in range(per_dev):
            for p in range(TILE):
                hit = sub_r == lax.shift_right_logical(target_line(chunk * TILE + p), shift_bits)
                parts = split_parts(ARR[chunk * TILE + p, k])
                for n, part in enumerate(parts):
                    for u in range(variables):
                        start = (n * variables + u) * rows
                        LHS[start : start + rows, p * slots : (p + 1) * slots] = jnp.where(
                            hit, part[u : u + 1, :].astype(jnp.float32), 0.0
                        ).astype(jnp.bfloat16)
            terms = lax.dot_general(
                LHS[...], COL[...], (((1,), (1,)), ((), ())), preferred_element_type=jnp.float32
            )
            height = variables * rows
            summed = terms[:height]
            for part in range(1, PARTS):
                summed = summed + terms[part * height : (part + 1) * height]
            SP[k] = SP[k] - summed.reshape(variables, rows, width)

    @pl.loop(2, nb - 2)
    def _(t):
        forward(t)

    for copy in loads[3:]:
        copy.wait()

    @pl.when(has_below)
    def _():
        halo_up(0).wait_recv()
        halo_face().wait_recv()

    @pl.when(has_above)
    def _():
        halo_down(0).wait_recv()

    d1, d2, d3 = (spectral_entry(d, instances) for d in (1, 2, 3))
    is_odd = odd == 1

    def pick(even_value, odd_value):
        return jnp.where(is_odd, jnp.float32(odd_value), jnp.float32(even_value))

    nxt = ((d2, d3), (d1, d2))
    prv = ((-d2, -d1), (-d3, -d2))
    c_sib = [[pick(nxt[g][m], prv[g][m]) for m in range(2)] for g in range(2)]
    c_rel = [[pick(prv[g][m], nxt[g][m]) for m in range(2)] for g in range(2)]
    c_own = (d1, -d1)
    c_x = (-d3, d3)

    sub8 = lax.broadcasted_iota(jnp.int32, (TILE, width), 0)
    lane8 = lax.broadcasted_iota(jnp.int32, (TILE, width), 1)

    @pl.loop(0, total)
    def _(t):
        sweep, block, row = place(t)
        here = pl.ds(row, TILE)
        mid = pl.ds(row + TILE, TILE)
        low = pl.ds(row, TILE)
        high = pl.ds(row + 2 * TILE, TILE)

        @pl.when(t < 2)
        def _():
            forward(t + nb - 2)

        @pl.when(t == nb)
        def _():
            forward(t)

        @pl.when((t >= nb) & (t + WINDOW < total))
        def _():
            x_copy(t + WINDOW).start()

        @pl.when((t >= nb) & (t + 1 < total))
        def _():
            forward(t + 1)

        @pl.when(t == nb)
        def _():
            @pl.when(has_below)
            def _():
                halo_up(1).wait_recv()

            @pl.when(has_above)
            def _():
                halo_down(1).wait_recv()

        sib_copy(t).wait_recv()
        relay_copy(t).wait_recv()
        scaled = freq[0] * VOL[here, :]

        for k in range(per_dev):
            other = 1 - k
            acc = []
            for u in range(variables):
                s = c_own[k] * A[sweep, other, u, mid, :] + c_x[k] * RX[sweep, other, u, here, :]
                for m in range(2):
                    s = s + c_sib[k][m] * SB[sweep, m, u, here, :]
                    s = s + c_rel[k][m] * RL[sweep, m, u, here, :]
                acc.append(SP[k, u, here, :] - scaled * s)
            fs_low = jnp.where(sub8 == TILE - 1, FS[k, low, :], FS[k, mid, :])
            fs_mid = FS[k, mid, :]
            fp = jnp.where(lane8 == width - 1, 0.0, FP[k, here, :])
            for v in range(variables):
                a = A[sweep, k, v, mid, :]
                x = pltpu.roll(
                    fs_low * jnp.where(sub8 == TILE - 1, A[sweep, k, v, low, :], a), 1, 0
                )
                y = fs_mid * pltpu.roll(
                    jnp.where(sub8 == 0, A[sweep, k, v, high, :], a), TILE - 1, 0
                )
                left = pltpu.roll(fp * a, 1, 1)
                right = fp * pltpu.roll(a, width - 1, 1)
                for u in range(variables):
                    acc[u] = acc[u] - (
                        (blocks[0, v, u] * x + blocks[1, v, u] * y)
                        + (blocks[2, v, u] * left + blocks[3, v, u] * right)
                    )
            scale = DS[k, here, :]
            for u in range(variables):
                R[k, u, here, :] = acc[u]
            for u in range(variables):
                new = dinv[k, u, 0] * acc[0]
                for v in range(1, variables):
                    new = new + dinv[k, u, v] * acc[v]
                A[sweep + 1, k, u, mid, :] = scale * new

        @pl.when(sweep == 0)
        def _():
            sib_copy(t + nb).start()

            @pl.when(t < WINDOW)
            def _():
                x_copy(t + nb).start()

        @pl.when(t == 1)
        def _():
            @pl.when(has_above)
            def _():
                halo_up(1).start()

            @pl.when(has_below)
            def _():
                halo_down(1).start()

        @pl.when(sweep == SWEEPS - 1)
        def _():
            pltpu.make_async_copy(
                A.at[SWEEPS, :, :, mid, :], out_a.at[:, :, here, :], oa.at[block]
            ).start()
            pltpu.make_async_copy(
                R.at[:, :, here, :], out_r.at[:, :, here, :], orr.at[block]
            ).start()

    @pl.loop(0, total)
    def _(t):
        relay_copy(t).wait_send()
        sib_copy(t).wait_send()

    p_x.wait_send()
    p_sib.wait_send()
    p_rel.wait_send()

    @pl.loop(1, n_space)
    def _(j):
        a2a(j).wait_send()

    @pl.when(has_above)
    def _():
        for sweep in range(SWEEPS):
            halo_up(sweep).wait_send()
        halo_face().wait_send()

    @pl.when(has_below)
    def _():
        for sweep in range(SWEEPS):
            halo_down(sweep).wait_send()

    @pl.loop(0, nb)
    def _(b):
        here = pl.ds(pl.multiple_of(b * TILE, TILE), TILE)
        mid = pl.ds(pl.multiple_of(b * TILE, TILE) + TILE, TILE)
        pltpu.make_async_copy(
            A.at[SWEEPS, :, :, mid, :], out_a.at[:, :, here, :], oa.at[b]
        ).wait()
        pltpu.make_async_copy(R.at[:, :, here, :], out_r.at[:, :, here, :], orr.at[b]).wait()


def body(n_space, *args):
    per_dev, variables, rows, width = args[0].shape
    slots = args[11].shape[2]
    nb = rows // TILE
    chunks = n_space // TILE
    total = SWEEPS * nb
    f32 = jnp.float32
    hbm = pl.BlockSpec(memory_space=pl.ANY)
    smem = pl.BlockSpec(memory_space=pltpu.SMEM)
    vmem = pl.BlockSpec(memory_space=pltpu.VMEM)
    dma = pltpu.SemaphoreType.DMA
    field = (per_dev, variables, rows, width)
    out = jax.ShapeDtypeStruct(field, f32)
    return pl.pallas_call(
        functools.partial(kernel, n_space),
        out_shape=(out, out),
        in_specs=[hbm] * 6 + [smem] * 5 + [vmem] * 3 + [smem],
        out_specs=(hbm, hbm),
        scratch_shapes=[
            pltpu.VMEM((SWEEPS + 1, per_dev, variables, rows + 2 * TILE, width), f32),
            pltpu.VMEM(field, f32),
            pltpu.VMEM(field, f32),
            pltpu.VMEM((per_dev, rows + TILE, width), f32),
            pltpu.VMEM((per_dev, rows, width), f32),
            pltpu.VMEM((per_dev, rows, width), f32),
            pltpu.VMEM((rows, width), f32),
            pltpu.VMEM((SWEEPS,) + field, f32),
            pltpu.VMEM((SWEEPS,) + field, f32),
            pltpu.VMEM((SWEEPS,) + field, f32),
            pltpu.VMEM((width, TILE * slots), jnp.bfloat16),
            pltpu.VMEM((per_dev, variables, chunks, TILE, slots), f32),
            pltpu.VMEM((4, per_dev, variables, chunks, TILE, slots), f32),
            pltpu.VMEM((n_space, per_dev, variables, slots), f32),
            pltpu.VMEM((n_space, per_dev, variables, slots), f32),
            pltpu.VMEM((PARTS * variables * rows, TILE * slots), jnp.bfloat16),
            dma((6,)),
            dma((total,)),
            dma((total,)),
            dma((total,)),
            dma((total,)),
            dma((total,)),
            dma((total,)),
            dma((2 * SWEEPS + 1,)),
            dma((2 * SWEEPS + 1,)),
            dma((3,)),
            dma((3,)),
            dma((n_space,)),
            dma((n_space,)),
            dma((nb,)),
            dma((nb,)),
        ],
        compiler_params=pltpu.CompilerParams(
            collective_id=0, has_side_effects=True, vmem_limit_bytes=56 * 1024 * 1024
        ),
    )(*args)


def solution(mesh):
    in_specs = (
        P("inst", None, "space", None),
        P("inst", None, "space", None),
        P("inst", "space", None),
        P("inst", "space", None),
        P("inst", "space", None),
        P("space", None),
        P(),
        P("inst", None, None),
        P(),
        P(),
        P(),
        P("space", None, None),
        P(None, "space", None),
        P("space", None, None),
        P("space", None),
    )
    out_specs = (P("inst", None, "space", None), P("inst", None, "space", None))
    return jax.shard_map(
        functools.partial(body, mesh.shape["space"]),
        mesh=mesh,
        in_specs=in_specs,
        out_specs=out_specs,
        check_vma=False,
    )
```

profile of v0, /device:TPU:0, one launch (start us, length us, event | category | flops | bytes accessed | tf_op | source)
XLA Modules:
  0.0 97.7 jit_solution(10347048071349502852)
XLA Ops:
  1.9 1.3 %copy.18.dinv = f32[2,6,6]{2,1,0:T(8,128)} copy(f32[2,6,6]{2,0,1:T(2,128)} %param.22) | data formatting | bytes 576 | tf_op args[7]
  3.2 1.3 %copy.17.blocks = f32[4,6,6]{2,1,0:T(8,128)} copy(f32[4,6,6]{2,0,1:T(4,128)} %param.21) | data formatting | bytes 1152 | tf_op args[6]
  4.5 89.3 %shard_map.158 = (f32[2,6,64,512]{3,2,1,0:T(8,128)}, f32[2,6,64,512]{3,2,1,0:T(8,128)}) custom-call(f32[2,6,64,512]{3,2,1,0:T(8,128)} %a_hbm.1, f32[2,6,64,512]{3,2,1,0:T(8,128)} %s_hbm.1, f32[2,64,512]{2,1,0:T(8,128)} %fs_hbm.1, f32[2,64,512]{2,1,0:T(8,128)} %fp_hbm.1, f32[2,64,512]{2,1,0:T(8,128)} %ds_hbm.1, f32[64,512]{1,0:T(8,128)} %vol_hbm.1, ...), custom_call_target="tpu_custom_call" | custom-call | tf_op jit(solution)/shard_map/pallas_call | solution.py:527
  93.8 0.0 copy-start
  93.8 2.8 %copy.23 = f32[2,6,64,512]{3,2,1,0:T(8,128)} copy(f32[2,6,64,512]{3,2,1,0:T(8,128)} %get-tuple-element.4) | data formatting | bytes 3145728
  96.6 0.0 copy-done
  96.6 1.1 %copy.24 = f32[2,6,64,512]{3,2,1,0:T(8,128)} copy(f32[2,6,64,512]{3,2,1,0:T(8,128)S(1)} %copy-done) | data formatting | bytes 3145728
Async XLA Ops:
  93.8 2.8 %copy-start = (f32[2,6,64,512]{3,2,1,0:T(8,128)S(1)}, f32[2,6,64,512]{3,2,1,0:T(8,128)}, u32[]{:S(2)}) copy-start(f32[2,6,64,512]{3,2,1,0:T(8,128)} %get-tuple-element.5) | copy-start | bytes 4718596
where the time goes:
time: 98.2 us; the launch traced here: 97.7 us
  Pallas kernels  89.3 us (91%)
  local copies, waits for them, and re-layouts  6.54 us (7%)
  between operations  1.94 us (2%)
    pallas_call x1, Pallas kernels, body(): pl.pallas_call(functools.partial(kernel, n_space), out_shape=(out, out),...  89.3 us
    unnamed x6, local copies, waits for them, and re-layouts  6.54 us

commit v1 on v0

v1 whole, which is shorter than its diff:
```python
import functools
import math

import jax
import jax.numpy as jnp
from jax import lax
from jax.experimental import pallas as pl
from jax.experimental.pallas import tpu as pltpu
from jax.sharding import PartitionSpec as P

SWEEPS = 2
TILE = 8
LANES = 128
PARTS = 2
CHUNK = 16
EARLY = 2
AHEAD = 2
LAG = 3
GROUP = 4
MESH = pl.DeviceIdType.MESH


def spectral_entry(offset, count):
    offset = offset % count
    if offset == 0 or 2 * offset == count:
        return 0.0
    return 0.5 * (-1.0) ** offset / math.tan(math.pi * offset / count)


def split_parts(value):
    parts = []
    for _ in range(PARTS):
        part = value.astype(jnp.bfloat16)
        parts.append(part)
        value = value - part.astype(jnp.float32)
    return parts


def kernel(
    n_space,
    n_inst,
    a_hbm,
    s_hbm,
    fs_hbm,
    fp_hbm,
    ds_hbm,
    vol_hbm,
    blocks,
    dinv,
    pblock,
    freq,
    shift,
    cells,
    targets,
    weights,
    counts,
    out_r,
    A,
    SP,
    AT,
    ST,
    RT,
    FS,
    FP,
    DS,
    VOL,
    CL,
    CR,
    PW,
    PF,
    DV,
    DT,
    COL,
    PICK,
    ALLP,
    ROUTED,
    ARR,
    LHS,
    load_sem,
    own_s,
    own_r,
    a_s,
    a_r,
    c_s,
    c_r,
    s_s,
    s_r,
    r_s,
    r_r,
    d_s,
    d_r,
    cols_s,
    cols_r,
    hs,
    hr,
    ps,
    pr,
    q_s,
    q_r,
):
    per_dev, variables, rows, width = a_hbm.shape
    instances = n_inst * per_dev
    cols = width // n_inst
    slots = cells.shape[2]
    nb = rows // TILE
    na = rows // CHUNK
    inst = lax.axis_index("inst")
    me = lax.axis_index("space")
    odd = inst % 2
    sibling = inst + 1 - 2 * odd
    across = (inst + 2) % n_inst
    shift_bits = width.bit_length() - 1
    peers = (2, 1, 3)

    def remote(src, dst, send, recv, **device):
        return pltpu.make_async_remote_copy(
            src_ref=src, dst_ref=dst, send_sem=send, recv_sem=recv, device_id=device,
            device_id_type=MESH,
        )

    def columns(i):
        return pl.ds(pl.multiple_of(i * cols, cols), cols)

    def members(i):
        return pl.ds(i * per_dev, per_dev)

    def local(src, dst, n):
        return pltpu.make_async_copy(src, dst, load_sem.at[n])

    inner = pl.ds(TILE, rows)
    mine = columns(inst)
    own = members(inst)
    loads = [
        local(a_hbm, A, 0),
        local(s_hbm, SP, 1),
        local(a_hbm.at[:, :, :, mine], AT.at[0, own, :, inner, :], 2),
        local(fp_hbm.at[:, :, mine], FP.at[own], 3),
        local(fs_hbm.at[:, :, mine], FS.at[own, inner, :], 4),
        local(ds_hbm.at[:, :, mine], DS.at[own], 5),
        local(vol_hbm.at[:, mine], VOL, 6),
    ]
    for copy in loads:
        copy.start()

    barrier = pltpu.get_barrier_semaphore()
    for d in peers:
        pl.semaphore_signal(
            barrier, inc=1, device_id={"inst": (inst + d) % n_inst}, device_id_type=MESH
        )

    @pl.loop(1, n_space)
    def _(j):
        pl.semaphore_signal(
            barrier, inc=1, device_id={"space": (me + j) % n_space}, device_id_type=MESH
        )

    def to(d):
        return (inst + d) % n_inst

    def source(d):
        return (inst + n_inst - d) % n_inst

    def a_copy(d, c, sender, receiver):
        span = pl.multiple_of(c * CHUNK, CHUNK)
        return remote(
            a_hbm.at[:, :, pl.ds(span, CHUNK), columns(receiver)],
            AT.at[0, members(sender), :, pl.ds(span + TILE, CHUNK), :],
            a_s.at[d - 1, c], a_r.at[d - 1, c], inst=receiver,
        )

    def fp_copy(d, sender, receiver):
        return remote(
            fp_hbm.at[:, :, columns(receiver)], FP.at[members(sender)],
            c_s.at[d - 1, 0], c_r.at[d - 1, 0], inst=receiver,
        )

    def fs_copy(d, sender, receiver):
        return remote(
            fs_hbm.at[:, :, columns(receiver)], FS.at[members(sender), inner, :],
            c_s.at[d - 1, 1], c_r.at[d - 1, 1], inst=receiver,
        )

    def ds_copy(d, sender, receiver):
        return remote(
            ds_hbm.at[:, :, columns(receiver)], DS.at[members(sender)],
            c_s.at[d - 1, 2], c_r.at[d - 1, 2], inst=receiver,
        )

    def dv_copy(d, sender, receiver):
        return remote(
            DV.at[sender], DV.at[sender], d_s.at[d - 1], d_r.at[d - 1], inst=receiver
        )

    def order(n):
        return (n + nb - 1) % nb

    def s_copy(d, n, sender, receiver):
        row = pl.multiple_of(order(n) * TILE, TILE)
        return remote(
            SP.at[:, :, pl.ds(row, TILE), columns(receiver)],
            ST.at[members(sender), :, pl.ds(row, TILE), :],
            s_s.at[d - 1, n], s_r.at[d - 1, n], inst=receiver,
        )

    def r_copy(d, b, sender, receiver):
        row = pl.multiple_of(b * TILE, TILE)
        return remote(
            RT.at[members(receiver), :, pl.ds(row, TILE), :],
            out_r.at[:, :, pl.ds(row, TILE), columns(sender)],
            r_s.at[d - 1, b], r_r.at[d - 1, b], inst=receiver,
        )

    def s_own(n):
        row = pl.multiple_of(order(n) * TILE, TILE)
        return pltpu.make_async_copy(
            SP.at[:, :, pl.ds(row, TILE), mine], ST.at[own, :, pl.ds(row, TILE), :], own_s.at[n]
        )

    def r_own(b):
        row = pl.multiple_of(b * TILE, TILE)
        return pltpu.make_async_copy(
            RT.at[own, :, pl.ds(row, TILE), :], out_r.at[:, :, pl.ds(row, TILE), mine],
            own_r.at[b],
        )

    def start(copy, *args):
        for d in peers:
            copy(d, *args, inst, to(d)).start()

    def arrived(copy, *args):
        for d in peers:
            copy(d, *args, source(d), inst).wait_recv()

    def sent(copy, *args):
        for d in peers:
            copy(d, *args, inst, to(d)).wait_send()

    has_above = me < n_space - 1
    has_below = me > 0
    above = (me + 1) % n_space
    below = (me + n_space - 1) % n_space
    has_left = inst > 0
    has_right = inst < n_inst - 1
    left_dev = (inst + n_inst - 1) % n_inst
    right_dev = (inst + 1) % n_inst

    def halo_up(sweep):
        return remote(
            AT.at[sweep, :, :, pl.ds(rows, TILE), :],
            AT.at[sweep, :, :, pl.ds(0, TILE), :],
            hs.at[2 * sweep], hr.at[2 * sweep], space=above,
        )

    def halo_down(sweep):
        return remote(
            AT.at[sweep, :, :, pl.ds(TILE, TILE), :],
            AT.at[sweep, :, :, pl.ds(rows + TILE, TILE), :],
            hs.at[2 * sweep + 1], hr.at[2 * sweep + 1], space=below,
        )

    def halo_face():
        last = 2 * SWEEPS
        return remote(
            FS.at[:, pl.ds(rows, TILE), :], FS.at[:, pl.ds(0, TILE), :],
            hs.at[last], hr.at[last], space=above,
        )

    def col_right(sweep, span, n):
        return remote(
            PW.at[sweep, span], CL.at[sweep, span], cols_s.at[0, n], cols_r.at[0, n],
            inst=right_dev,
        )

    def col_left(sweep, span, n):
        return remote(
            PF.at[sweep, span], CR.at[sweep, span], cols_s.at[1, n], cols_r.at[1, n],
            inst=left_dev,
        )

    def zeros(*shape):
        return jnp.zeros(shape, jnp.float32)

    @pl.when(me == 0)
    def _():
        FS[:, 0:TILE, :] = zeros(instances, TILE, cols)
        for sweep in range(SWEEPS):
            AT[sweep, :, :, 0:TILE, :] = zeros(instances, variables, TILE, cols)

    @pl.when(me == n_space - 1)
    def _():
        for sweep in range(SWEEPS):
            AT[sweep, :, :, rows + TILE : rows + 2 * TILE, :] = zeros(
                instances, variables, TILE, cols
            )

    @pl.when(inst == 0)
    def _():
        CL[...] = zeros(SWEEPS, rows, cols)

    @pl.when(inst == n_inst - 1)
    def _():
        CR[...] = zeros(SWEEPS, rows, cols)

    sub8 = lax.broadcasted_iota(jnp.int32, (TILE, cols), 0)
    lane8 = lax.broadcasted_iota(jnp.int32, (TILE, cols), 1)

    packed = zeros(TILE, cols)
    for k in range(per_dev):
        for u in range(variables):
            for v in range(variables):
                n = (k * variables + u) * variables + v
                packed = jnp.where(lane8 == n, dinv[u, k, v], packed)
    DV[inst] = packed

    pl.semaphore_wait(barrier, n_space + n_inst - 2)

    for c in range(min(EARLY, na)):
        start(a_copy, c)
    start(dv_copy)

    sub_w = lax.broadcasted_iota(jnp.int32, (width, slots), 0)
    sub_r = lax.broadcasted_iota(jnp.int32, (rows, slots), 0)

    def column_table(index, chunk):
        for q in range(TILE):
            line = index(chunk * TILE + q)
            column = jnp.bitwise_and(line, width - 1)
            hot = jnp.where(sub_w == column, 1.0, 0.0).astype(jnp.bfloat16)
            COL[:, q * slots : (q + 1) * slots] = hot

    def cell_line(q):
        return cells[0, pl.ds(q, 1), :]

    def target_line(p):
        return targets[p, 0:1, :]

    chunks = n_space // TILE

    loads[0].wait()

    @pl.loop(0, chunks)
    def _(chunk):
        column_table(cell_line, chunk)

        @pl.loop(0, per_dev)
        def _(k):
            field = A[k].reshape(variables * rows, width)
            stacked = jnp.concatenate(split_parts(field), axis=0)
            terms = jnp.dot(stacked, COL[...], preferred_element_type=jnp.float32)
            height = variables * rows
            found = terms[:height]
            for part in range(1, PARTS):
                found = found + terms[part * height : (part + 1) * height]
            for q in range(TILE):
                hit = sub_r == lax.shift_right_logical(cell_line(chunk * TILE + q), shift_bits)
                for v in range(variables):
                    piece = found[v * rows : (v + 1) * rows, q * slots : (q + 1) * slots]
                    PICK[k, v, chunk, q : q + 1, :] = jnp.sum(
                        jnp.where(hit, piece, 0.0), axis=0, keepdims=True
                    )

        lane = lax.broadcasted_iota(jnp.int32, (TILE, slots), 1)
        sub = lax.broadcasted_iota(jnp.int32, (TILE, slots), 0)
        limit = jnp.zeros((TILE, slots), jnp.int32)
        for q in range(TILE):
            limit = jnp.where(sub == q, counts[0, chunk * TILE + q], limit)
        first = pl.multiple_of(chunk * TILE, TILE)
        weight = jnp.where(lane < limit, weights[0, pl.ds(first, TILE), :], 0.0)

        for k in range(per_dev):
            picked = [PICK[k, v, chunk] for v in range(variables)]
            for u in range(variables):
                mixed = pblock[0, u] * picked[0]
                for v in range(1, variables):
                    mixed = mixed + pblock[v, u] * picked[v]
                ALLP[0, k, u, chunk] = mixed * weight

    p_x = remote(ALLP.at[0], ALLP.at[2], ps.at[0], pr.at[0], inst=across)
    p_sib = remote(ALLP.at[0], ALLP.at[3 - 2 * odd], ps.at[1], pr.at[1 + odd], inst=sibling)
    p_rel = remote(ALLP.at[2], ALLP.at[1 + 2 * odd], ps.at[2], pr.at[2 - odd], inst=sibling)
    p_sib_in = remote(ALLP.at[0], ALLP.at[1 + 2 * odd], ps.at[1], pr.at[2 - odd], inst=sibling)
    p_rel_in = remote(ALLP.at[2], ALLP.at[3 - 2 * odd], ps.at[2], pr.at[1 + odd], inst=sibling)
    p_x.start()
    p_sib.start()
    start(fp_copy)
    for c in range(min(EARLY, na), na):
        start(a_copy, c)
    start(fs_copy)
    start(ds_copy)
    p_x.wait_recv()
    p_rel.start()
    p_sib_in.wait_recv()
    p_rel_in.wait_recv()
    for k in range(per_dev):
        wanted = lax.rem(k - shift[0] + 2 * instances, instances)
        group = lax.div(wanted, per_dev)
        member = lax.rem(wanted, per_dev)

        @pl.loop(0, chunks)
        def _(chunk):
            for u in range(variables):
                value = ALLP[group, member, u, chunk]
                for q in range(TILE):
                    ROUTED[chunk * TILE + q, k, u : u + 1, :] = value[q : q + 1, :]

    def a2a(j):
        return remote(
            ROUTED.at[(me + j) % n_space], ARR.at[me], q_s.at[j], q_r.at[j],
            space=(me + j) % n_space,
        )

    @pl.loop(1, n_space)
    def _(j):
        a2a(j).start()

    ARR[me] = ROUTED[me]
    loads[1].wait()
    column_table(target_line, 0)

    @pl.loop(1, n_space)
    def _(j):
        remote(
            ROUTED.at[0], ARR.at[(me + n_space - j) % n_space], q_s.at[j], q_r.at[j],
            space=(me + j) % n_space,
        ).wait_recv()

    @pl.loop(0, chunks)
    def _(chunk):
        if chunks > 1:
            column_table(target_line, chunk)

        for k in range(per_dev):
            for p in range(TILE):
                hit = sub_r == lax.shift_right_logical(target_line(chunk * TILE + p), shift_bits)
                parts = split_parts(ARR[chunk * TILE + p, k])
                for n, part in enumerate(parts):
                    for u in range(variables):
                        begin = (n * variables + u) * rows
                        LHS[begin : begin + rows, p * slots : (p + 1) * slots] = jnp.where(
                            hit, part[u : u + 1, :].astype(jnp.float32), 0.0
                        ).astype(jnp.bfloat16)
            terms = lax.dot_general(
                LHS[...], COL[...], (((1,), (1,)), ((), ())), preferred_element_type=jnp.float32
            )
            height = variables * rows
            summed = terms[:height]
            for part in range(1, PARTS):
                summed = summed + terms[part * height : (part + 1) * height]
            SP[k] = SP[k] - summed.reshape(variables, rows, width)

    for copy in loads[2:]:
        copy.wait()
    arrived(fp_copy)

    @pl.loop(0, na)
    def _(c):
        arrived(a_copy, c)

    @pl.when(has_above)
    def _():
        halo_up(0).start()

    @pl.when(has_below)
    def _():
        halo_down(0).start()

    def pack(sweep, row):
        here = pl.ds(row, TILE)
        mid = pl.ds(row + TILE, TILE)
        last = zeros(TILE, cols)
        first = zeros(TILE, cols)
        for g in range(instances):
            fp = FP[g, here, :]
            for v in range(variables):
                n = g * variables + v
                a = AT[sweep, g, v, mid, :]
                first = jnp.where(lane8 == n, pltpu.roll(a, n, 1) if n else a, first)
                last = jnp.where(lane8 == n, pltpu.roll(fp * a, n + 1, 1), last)
        PW[sweep, here, :] = last
        PF[sweep, here, :] = first

    @pl.loop(0, nb)
    def _(b):
        pack(0, pl.multiple_of(b * TILE, TILE))

    whole = pl.ds(0, rows)

    @pl.when(has_right)
    def _():
        col_right(0, whole, nb).start()

    @pl.when(has_left)
    def _():
        col_left(0, whole, nb).start()

    for n in range(AHEAD):
        start(s_copy, n)

    @pl.loop(0, nb)
    def _(n):
        s_own(n).start()

    arrived(dv_copy)
    for g in range(instances):
        vector = DV[g // per_dev]
        for n in range(variables * variables):
            lane = (g % per_dev) * variables * variables + n
            DT[g * variables * variables + n] = jnp.broadcast_to(
                vector[:, lane : lane + 1], (TILE, cols)
            )

    arrived(fs_copy)

    @pl.when(has_above)
    def _():
        halo_face().start()

    arrived(ds_copy)

    @pl.when(has_below)
    def _():
        halo_up(0).wait_recv()
        halo_face().wait_recv()

    @pl.when(has_above)
    def _():
        halo_down(0).wait_recv()

    @pl.when(has_left)
    def _():
        col_right(0, whole, nb).wait_recv()

    @pl.when(has_right)
    def _():
        col_left(0, whole, nb).wait_recv()

    f1, f2, f3 = (spectral_entry(d, instances) for d in (1, 2, 3))

    def update(sweep, row):
        here = pl.ds(row, TILE)
        mid = pl.ds(row + TILE, TILE)
        low = pl.ds(row, TILE)
        high = pl.ds(row + 2 * TILE, TILE)
        scaled = freq[0] * VOL[here, :]
        v1 = (0.5 * (f1 - f3)) * scaled
        v2 = f2 * scaled
        v3 = (0.5 * (f1 + f3)) * scaled
        for u in range(variables):
            a = [AT[sweep, g, u, mid, :] for g in range(instances)]
            b = [a[g] - a[g + 4] for g in range(4)]
            c = [a[g] + a[g + 4] for g in range(4)]
            even = v1 * (c[1] - c[3])
            odds = v1 * (c[2] - c[0])
            q = [even, odds, -even, -odds]
            p = [
                v2 * b[2] + v3 * (b[1] + b[3]),
                v2 * b[3] + v3 * (b[2] - b[0]),
                v3 * (b[3] - b[1]) - v2 * b[0],
                -(v2 * b[1] + v3 * (b[0] + b[2])),
            ]
            for g in range(4):
                RT[g, u, here, :] = ST[g, u, here, :] - (q[g] + p[g])
                RT[g + 4, u, here, :] = ST[g + 4, u, here, :] - (q[g] - p[g])
        top = sub8 == TILE - 1
        bottom = sub8 == 0
        for base in range(0, instances, GROUP):
            span = range(base, base + GROUP)
            acc = {(g, u): RT[g, u, here, :] for g in span for u in range(variables)}
            fm = {g: FS[g, mid, :] for g in span}
            fl = {g: jnp.where(top, FS[g, low, :], fm[g]) for g in span}
            fp = {g: FP[g, here, :] for g in span}
            cl = CL[sweep, here, :]
            cr = CR[sweep, here, :]
            for v in range(variables):
                terms = {}
                for g in span:
                    n = g * variables + v
                    a = AT[sweep, g, v, mid, :]
                    x = pltpu.roll(fl[g] * jnp.where(top, AT[sweep, g, v, low, :], a), 1, 0)
                    y = fm[g] * pltpu.roll(
                        jnp.where(bottom, AT[sweep, g, v, high, :], a), TILE - 1, 0
                    )
                    edge = pltpu.roll(cl, cols - n, 1) if n else cl
                    left = jnp.where(lane8 == 0, edge, pltpu.roll(fp[g] * a, 1, 1))
                    edge = pltpu.roll(cr, cols - 1 - n, 1)
                    right = fp[g] * jnp.where(
                        lane8 == cols - 1, edge, pltpu.roll(a, cols - 1, 1)
                    )
                    terms[g] = (x, y, left, right)
                for u in range(variables):
                    k0, k1, k2, k3 = (blocks[v, n, u] for n in range(4))
                    for g in span:
                        x, y, left, right = terms[g]
                        acc[g, u] = acc[g, u] - (
                            (k0 * x + k1 * y) + (k2 * left + k3 * right)
                        )
            if sweep == SWEEPS - 1:
                for g in span:
                    for u in range(variables):
                        RT[g, u, here, :] = acc[g, u]
            else:
                for g in span:
                    scale = DS[g, here, :]
                    for u in range(variables):
                        n = (g * variables + u) * variables
                        new = DT[n] * acc[g, 0]
                        for v in range(1, variables):
                            new = new + DT[n + v] * acc[g, v]
                        AT[sweep + 1, g, u, mid, :] = scale * new

    @pl.loop(0, nb + LAG)
    def _(n):
        @pl.when(n < nb)
        def _():
            row = pl.multiple_of(order(n) * TILE, TILE)
            s_own(n).wait()
            arrived(s_copy, n)

            @pl.when(n + AHEAD < nb)
            def _():
                start(s_copy, n + AHEAD)

            update(0, row)
            pack(1, row)
            span = pl.ds(row, TILE)

            @pl.when(has_right)
            def _():
                col_right(1, span, order(n)).start()

            @pl.when(has_left)
            def _():
                col_left(1, span, order(n)).start()

        @pl.when(n == 1)
        def _():
            @pl.when(has_above)
            def _():
                halo_up(1).start()

            @pl.when(has_below)
            def _():
                halo_down(1).start()

        @pl.when(n == LAG)
        def _():
            @pl.when(has_below)
            def _():
                halo_up(1).wait_recv()

            @pl.when(has_above)
            def _():
                halo_down(1).wait_recv()

        @pl.when(n >= LAG)
        def _():
            b = n - LAG
            row = pl.multiple_of(b * TILE, TILE)
            span = pl.ds(row, TILE)

            @pl.when(has_left)
            def _():
                col_right(1, span, b).wait_recv()

            @pl.when(has_right)
            def _():
                col_left(1, span, b).wait_recv()

            update(1, row)
            start(r_copy, b)
            r_own(b).start()

    start_list = (fp_copy, fs_copy, ds_copy, dv_copy)
    for copy in start_list:
        sent(copy)

    @pl.loop(0, na)
    def _(c):
        sent(a_copy, c)

    p_x.wait_send()
    p_sib.wait_send()
    p_rel.wait_send()

    @pl.loop(1, n_space)
    def _(j):
        a2a(j).wait_send()

    @pl.when(has_above)
    def _():
        for sweep in range(SWEEPS):
            halo_up(sweep).wait_send()
        halo_face().wait_send()

    @pl.when(has_below)
    def _():
        for sweep in range(SWEEPS):
            halo_down(sweep).wait_send()

    @pl.when(has_right)
    def _():
        col_right(0, whole, nb).wait_send()

    @pl.when(has_left)
    def _():
        col_left(0, whole, nb).wait_send()

    @pl.loop(0, nb)
    def _(b):
        span = pl.ds(pl.multiple_of(b * TILE, TILE), TILE)

        @pl.when(has_right)
        def _():
            col_right(1, span, b).wait_send()

        @pl.when(has_left)
        def _():
            col_left(1, span, b).wait_send()

        sent(s_copy, b)
        sent(r_copy, b)
        r_own(b).wait()
        arrived(r_copy, b)


def finish(dinv, r, ds, out_a, out_r):
    per_dev, variables = r.shape[:2]
    for k in range(per_dev):
        scale = ds[k]
        rest = [r[k, v] for v in range(variables)]
        for u in range(variables):
            out_r[k, u] = rest[u]
            new = dinv[u, k, 0] * rest[0]
            for v in range(1, variables):
                new = new + dinv[u, k, v] * rest[v]
            out_a[k, u] = scale * new


def body(n_space, n_inst, a, s, fs, fp, ds, vol, blocks, dinv, *rest):
    per_dev, variables, rows, width = a.shape
    slots = rest[3].shape[2]
    nb = rows // TILE
    na = rows // CHUNK
    chunks = n_space // TILE
    instances = n_inst * per_dev
    cols = width // n_inst
    f32 = jnp.float32
    hbm = pl.BlockSpec(memory_space=pl.ANY)
    smem = pl.BlockSpec(memory_space=pltpu.SMEM)
    vmem = pl.BlockSpec(memory_space=pltpu.VMEM)
    dma = pltpu.SemaphoreType.DMA
    field = (per_dev, variables, rows, width)
    out = jax.ShapeDtypeStruct(field, f32)
    moved = (instances, variables, rows, cols)
    blocks = jnp.transpose(blocks, (1, 0, 2))
    dinv = jnp.transpose(dinv, (1, 0, 2))
    r = pl.pallas_call(
        functools.partial(kernel, n_space, n_inst),
        out_shape=out,
        in_specs=[hbm] * 6 + [smem] * 5 + [vmem] * 3 + [smem],
        out_specs=hbm,
        scratch_shapes=[
            pltpu.VMEM(field, f32),
            pltpu.VMEM(field, f32),
            pltpu.VMEM((SWEEPS, instances, variables, rows + 2 * TILE, cols), f32),
            pltpu.VMEM(moved, f32),
            pltpu.VMEM(moved, f32),
            pltpu.VMEM((instances, rows + TILE, cols), f32),
            pltpu.VMEM((instances, rows, cols), f32),
            pltpu.VMEM((instances, rows, cols), f32),
            pltpu.VMEM((rows, cols), f32),
            pltpu.VMEM((SWEEPS, rows, cols), f32),
            pltpu.VMEM((SWEEPS, rows, cols), f32),
            pltpu.VMEM((SWEEPS, rows, cols), f32),
            pltpu.VMEM((SWEEPS, rows, cols), f32),
            pltpu.VMEM((n_inst, TILE, cols), f32),
            pltpu.VMEM((instances * variables * variables, TILE, cols), f32),
            pltpu.VMEM((width, TILE * slots), jnp.bfloat16),
            pltpu.VMEM((per_dev, variables, chunks, TILE, slots), f32),
            pltpu.VMEM((4, per_dev, variables, chunks, TILE, slots), f32),
            pltpu.VMEM((n_space, per_dev, variables, slots), f32),
            pltpu.VMEM((n_space, per_dev, variables, slots), f32),
            pltpu.VMEM((PARTS * variables * rows, TILE * slots), jnp.bfloat16),
            dma((7,)),
            dma((nb,)),
            dma((nb,)),
            dma((3, na)),
            dma((3, na)),
            dma((3, 3)),
            dma((3, 3)),
            dma((3, nb)),
            dma((3, nb)),
            dma((3, nb)),
            dma((3, nb)),
            dma((3,)),
            dma((3,)),
            dma((2, nb + 1)),
            dma((2, nb + 1)),
            dma((2 * SWEEPS + 1,)),
            dma((2 * SWEEPS + 1,)),
            dma((3,)),
            dma((3,)),
            dma((n_space,)),
            dma((n_space,)),
        ],
        compiler_params=pltpu.CompilerParams(
            collective_id=0, has_side_effects=True, vmem_limit_bytes=56 * 1024 * 1024
        ),
    )(a, s, fs, fp, ds, vol, blocks, dinv, *rest)
    block = pl.BlockSpec((per_dev, variables, CHUNK, width), lambda b: (0, 0, b, 0))
    return pl.pallas_call(
        finish,
        grid=(rows // CHUNK,),
        out_shape=(out, out),
        in_specs=[smem, block, pl.BlockSpec((per_dev, CHUNK, width), lambda b: (0, b, 0))],
        out_specs=(block, block),
    )(dinv, r, ds)


def solution(mesh):
    in_specs = (
        P("inst", None, "space", None),
        P("inst", None, "space", None),
        P("inst", "space", None),
        P("inst", "space", None),
        P("inst", "space", None),
        P("space", None),
        P(),
        P("inst", None, None),
        P(),
        P(),
        P(),
        P("space", None, None),
        P(None, "space", None),
        P("space", None, None),
        P("space", None),
    )
    out_specs = (P("inst", None, "space", None), P("inst", None, "space", None))
    return jax.shard_map(
        functools.partial(body, mesh.shape["space"], mesh.shape["inst"]),
        mesh=mesh,
        in_specs=in_specs,
        out_specs=out_specs,
        check_vma=False,
    )
```

time: 98.2 us -> 81.6 us (0.83)
  the two profiles are of different devices: /device:TPU:0 before, /device:TPU:8 now
where the time goes in v1:
time: 81.6 us; the launch traced here: 81.3 us
  Pallas kernels  79.4 us (97%)
  between operations  1.93 us (2%)
    pallas_call x1, Pallas kernels, body(): pl.pallas_call(functools.partial(kernel, n_space, n_inst), out_shape=out,...  75.2 us
    pallas_call x1, Pallas kernels, body(): pl.pallas_call(finish, grid=(rows // CHUNK,), out_shape=(out, out), in_sp...  4.2 us

profile of v1, /device:TPU:8, one launch (start us, length us, event | category | flops | bytes accessed | tf_op | source)
XLA Modules:
  0.0 81.3 jit_solution(7667303626435038253)
XLA Ops:
  1.9 75.2 %shard_map.158.r = f32[2,6,64,512]{3,2,1,0:T(8,128)} custom-call(f32[2,6,64,512]{3,2,1,0:T(8,128)} %a_hbm.1, f32[2,6,64,512]{3,2,1,0:T(8,128)} %s_hbm.1, f32[2,64,512]{2,1,0:T(8,128)} %fs_hbm.1, f32[2,64,512]{2,1,0:T(8,128)} %fp_hbm.1, f32[2,64,512]{2,1,0:T(8,128)} %ds.1, f32[64,512]{1,0:T(8,128)} %vol_hbm.1, f32[6,4,6]{2,1,0:T(4,128)} %bitcast.4, ...), custom_call_target="tpu_custom_call" | custom-call | tf_op jit(solution)/shard_map/pallas_call | solution.py:757
  77.1 4.2 %shard_map.159 = (f32[2,6,64,512]{3,2,1,0:T(8,128)}, f32[2,6,64,512]{3,2,1,0:T(8,128)}) custom-call(f32[6,2,6]{2,1,0:T(2,128)} %bitcast.3, f32[2,6,64,512]{3,2,1,0:T(8,128)} %shard_map.158.r, f32[2,64,512]{2,1,0:T(8,128)} %ds.1), custom_call_target="tpu_custom_call" | custom-call | tf_op jit(solution)/shard_map/pallas_call | solution.py:811

commit v2 on v1

--- a/solution.py
+++ b/solution.py
@@ -54,6 +54,7 @@
     targets,
     weights,
     counts,
+    out_a,
     out_r,
     A,
     SP,
@@ -64,6 +65,7 @@
     FP,
     DS,
     VOL,
+    DH,
     CL,
     CR,
     PW,
@@ -138,6 +140,7 @@
         local(fs_hbm.at[:, :, mine], FS.at[own, inner, :], 4),
         local(ds_hbm.at[:, :, mine], DS.at[own], 5),
         local(vol_hbm.at[:, mine], VOL, 6),
+        local(ds_hbm, DH, 7),
     ]
     for copy in loads:
         copy.start()
@@ -246,22 +249,22 @@
 
     def halo_up(sweep):
         return remote(
-            AT.at[sweep, :, :, pl.ds(rows, TILE), :],
-            AT.at[sweep, :, :, pl.ds(0, TILE), :],
+            AT.at[sweep, :, :, pl.ds(rows + TILE - 1, 1), :],
+            AT.at[sweep, :, :, pl.ds(TILE - 1, 1), :],
             hs.at[2 * sweep], hr.at[2 * sweep], space=above,
         )
 
     def halo_down(sweep):
         return remote(
-            AT.at[sweep, :, :, pl.ds(TILE, TILE), :],
-            AT.at[sweep, :, :, pl.ds(rows + TILE, TILE), :],
+            AT.at[sweep, :, :, pl.ds(TILE, 1), :],
+            AT.at[sweep, :, :, pl.ds(rows + TILE, 1), :],
             hs.at[2 * sweep + 1], hr.at[2 * sweep + 1], space=below,
         )
 
     def halo_face():
         last = 2 * SWEEPS
         return remote(
-            FS.at[:, pl.ds(rows, TILE), :], FS.at[:, pl.ds(0, TILE), :],
+            FS.at[:, pl.ds(rows + TILE - 1, 1), :], FS.at[:, pl.ds(TILE - 1, 1), :],
             hs.at[last], hr.at[last], space=above,
         )
 
@@ -670,8 +673,21 @@
             start(r_copy, b)
             r_own(b).start()
 
-    start_list = (fp_copy, fs_copy, ds_copy, dv_copy)
-    for copy in start_list:
+    @pl.loop(0, nb)
+    def _(b):
+        here = pl.ds(pl.multiple_of(b * TILE, TILE), TILE)
+        r_own(b).wait()
+        arrived(r_copy, b)
+        for k in range(per_dev):
+            scale = DH[k, here, :]
+            rest = [out_r[k, v, here, :] for v in range(variables)]
+            for u in range(variables):
+                new = dinv[u, k, 0] * rest[0]
+                for v in range(1, variables):
+                    new = new + dinv[u, k, v] * rest[v]
+                out_a[k, u, here, :] = scale * new
+
+    for copy in (fp_copy, fs_copy, ds_copy, dv_copy):
         sent(copy)
 
     @pl.loop(0, na)
@@ -719,21 +735,17 @@
 
         sent(s_copy, b)
         sent(r_copy, b)
-        r_own(b).wait()
-        arrived(r_copy, b)
-
-
-def finish(dinv, r, ds, out_a, out_r):
-    per_dev, variables = r.shape[:2]
-    for k in range(per_dev):
-        scale = ds[k]
-        rest = [r[k, v] for v in range(variables)]
-        for u in range(variables):
-            out_r[k, u] = rest[u]
-            new = dinv[u, k, 0] * rest[0]
-            for v in range(1, variables):
-                new = new + dinv[u, k, v] * rest[v]
-            out_a[k, u] = scale * new
+
+
+def finish(a, r, out_a, out_r, sems):
+    copies = [
+        pltpu.make_async_copy(a, out_a, sems.at[0]),
+        pltpu.make_async_copy(r, out_r, sems.at[1]),
+    ]
+    for copy in copies:
+        copy.start()
+    for copy in copies:
+        copy.wait()
 
 
 def body(n_space, n_inst, a, s, fs, fp, ds, vol, blocks, dinv, *rest):
@@ -754,11 +766,12 @@
     moved = (instances, variables, rows, cols)
     blocks = jnp.transpose(blocks, (1, 0, 2))
     dinv = jnp.transpose(dinv, (1, 0, 2))
-    r = pl.pallas_call(
+    placed = pltpu.VMEM(field, f32)
+    new, r = pl.pallas_call(
         functools.partial(kernel, n_space, n_inst),
-        out_shape=out,
+        out_shape=(placed, placed),
         in_specs=[hbm] * 6 + [smem] * 5 + [vmem] * 3 + [smem],
-        out_specs=hbm,
+        out_specs=(vmem, vmem),
         scratch_shapes=[
             pltpu.VMEM(field, f32),
             pltpu.VMEM(field, f32),
@@ -769,6 +782,7 @@
             pltpu.VMEM((instances, rows, cols), f32),
             pltpu.VMEM((instances, rows, cols), f32),
             pltpu.VMEM((rows, cols), f32),
+            pltpu.VMEM((per_dev, rows, width), f32),
             pltpu.VMEM((SWEEPS, rows, cols), f32),
             pltpu.VMEM((SWEEPS, rows, cols), f32),
             pltpu.VMEM((SWEEPS, rows, cols), f32),
@@ -781,7 +795,7 @@
             pltpu.VMEM((n_space, per_dev, variables, slots), f32),
             pltpu.VMEM((n_space, per_dev, variables, slots), f32),
             pltpu.VMEM((PARTS * variables * rows, TILE * slots), jnp.bfloat16),
-            dma((7,)),
+            dma((8,)),
             dma((nb,)),
             dma((nb,)),
             dma((3, na)),
@@ -807,14 +821,13 @@
             collective_id=0, has_side_effects=True, vmem_limit_bytes=56 * 1024 * 1024
         ),
     )(a, s, fs, fp, ds, vol, blocks, dinv, *rest)
-    block = pl.BlockSpec((per_dev, variables, CHUNK, width), lambda b: (0, 0, b, 0))
     return pl.pallas_call(
         finish,
-        grid=(rows // CHUNK,),
         out_shape=(out, out),
-        in_specs=[smem, block, pl.BlockSpec((per_dev, CHUNK, width), lambda b: (0, b, 0))],
-        out_specs=(block, block),
-    )(dinv, r, ds)
+        in_specs=[vmem, vmem],
+        out_specs=(hbm, hbm),
+        scratch_shapes=[dma((2,))],
+    )(*(pltpu.with_memory_space_constraint(x, pltpu.VMEM) for x in (new, r)))
 
 
 def solution(mesh):

time: 81.6 us -> 76.4 us (0.936)
  the two profiles are of different devices: /device:TPU:8 before, /device:TPU:0 now
where the time goes in v2:
time: 76.4 us; the launch traced here: 76.2 us
  Pallas kernels  74.3 us (97%)
  between operations  1.93 us (3%)
    pallas_call x1, Pallas kernels, body(): pl.pallas_call(functools.partial(kernel, n_space, n_inst), out_shape=(pla...  72.6 us
    pallas_call x1, Pallas kernels, body(): pl.pallas_call(finish, out_shape=(out, out), in_specs=[vmem, vmem], out_s...  1.68 us

profile of v2, /device:TPU:0, one launch (start us, length us, event | category | flops | bytes accessed | tf_op | source)
XLA Modules:
  0.0 76.2 jit_solution(10524779030713547184)
XLA Ops:
  1.9 72.6 %shard_map.158 = (f32[2,6,64,512]{3,2,1,0:T(8,128)S(1)}, f32[2,6,64,512]{3,2,1,0:T(8,128)S(1)}) custom-call(f32[2,6,64,512]{3,2,1,0:T(8,128)} %a_hbm.1, f32[2,6,64,512]{3,2,1,0:T(8,128)} %s_hbm.1, f32[2,64,512]{2,1,0:T(8,128)} %fs_hbm.1, f32[2,64,512]{2,1,0:T(8,128)} %fp_hbm.1, f32[2,64,512]{2,1,0:T(8,128)} %ds_hbm.1, f32[64,512]{1,0:T(8,128)} %vol_hbm.1, ...), custom_call_target="tpu_custom_call" | custom-call | tf_op jit(solution)/shard_map/pallas_call | solution.py:770
  74.5 1.7 %shard_map.159 = (f32[2,6,64,512]{3,2,1,0:T(8,128)}, f32[2,6,64,512]{3,2,1,0:T(8,128)}) custom-call(f32[2,6,64,512]{3,2,1,0:T(8,128)S(1)} %get-tuple-element.4.a, f32[2,6,64,512]{3,2,1,0:T(8,128)S(1)} %get-tuple-element.5.r), custom_call_target="tpu_custom_call" | custom-call | tf_op jit(solution)/shard_map/pallas_call | solution.py:824

commit v3 on v2

--- a/solution.py
+++ b/solution.py
@@ -99,6 +99,7 @@
     pr,
     q_s,
     q_r,
+    token,
 ):
     per_dev, variables, rows, width = a_hbm.shape
     instances = n_inst * per_dev
@@ -151,11 +152,26 @@
             barrier, inc=1, device_id={"inst": (inst + d) % n_inst}, device_id_type=MESH
         )
 
-    @pl.loop(1, n_space)
-    def _(j):
+    has_hi = me < n_space - 2
+    has_lo = me > 1
+    hi = (me + 2) % n_space
+    lo = (me + n_space - 2) % n_space
+    pair = me + 1 - 2 * (me % 2)
+
+    def greet(semaphore, device):
         pl.semaphore_signal(
-            barrier, inc=1, device_id={"space": (me + j) % n_space}, device_id_type=MESH
-        )
+            semaphore, inc=1, device_id={"space": device}, device_id_type=MESH
+        )
+
+    greet(barrier, pair)
+
+    @pl.when(has_hi)
+    def _():
+        greet(barrier, hi)
+
+    @pl.when(has_lo)
+    def _():
+        greet(barrier, lo)
 
     def to(d):
         return (inst + d) % n_inst
@@ -315,11 +331,19 @@
                 packed = jnp.where(lane8 == n, dinv[u, k, v], packed)
     DV[inst] = packed
 
-    pl.semaphore_wait(barrier, n_space + n_inst - 2)
+    pl.semaphore_wait(barrier, n_inst + has_hi.astype(jnp.int32) + has_lo.astype(jnp.int32))
 
     for c in range(min(EARLY, na)):
         start(a_copy, c)
     start(dv_copy)
+
+    @pl.when(jnp.logical_not(has_hi))
+    def _():
+        greet(token.at[0], lo)
+
+    @pl.when(jnp.logical_not(has_lo))
+    def _():
+        greet(token.at[1], hi)
 
     sub_w = lax.broadcasted_iota(jnp.int32, (width, slots), 0)
     sub_r = lax.broadcasted_iota(jnp.int32, (rows, slots), 0)
@@ -390,6 +414,23 @@
         start(a_copy, c)
     start(fs_copy)
     start(ds_copy)
+
+    @pl.when(has_hi)
+    def _():
+        pl.semaphore_wait(token.at[0], 1)
+
+        @pl.when(has_lo)
+        def _():
+            greet(token.at[0], lo)
+
+    @pl.when(has_lo)
+    def _():
+        pl.semaphore_wait(token.at[1], 1)
+
+        @pl.when(has_hi)
+        def _():
+            greet(token.at[1], hi)
+
     p_x.wait_recv()
     p_rel.start()
     p_sib_in.wait_recv()
@@ -816,6 +857,7 @@
             dma((3,)),
             dma((n_space,)),
             dma((n_space,)),
+            pltpu.SemaphoreType.REGULAR((2,)),
         ],
         compiler_params=pltpu.CompilerParams(
             collective_id=0, has_side_effects=True, vmem_limit_bytes=56 * 1024 * 1024

time: 76.4 us -> 73.4 us (0.961)
  Pallas kernels: 74.3 us -> 71.3 us
    pallas_call x1, Pallas kernels: 72.6 us -> 69.6 us  [body(): pl.pallas_call(functools.partial(kernel, n_space, n_inst), out_shape=(pla...]
where the time goes in v3:
time: 73.4 us; the launch traced here: 73.2 us
  Pallas kernels  71.3 us (97%)
  between operations  1.93 us (3%)
    pallas_call x1, Pallas kernels, body(): pl.pallas_call(functools.partial(kernel, n_space, n_inst), out_shape=(pla...  69.6 us
    pallas_call x1, Pallas kernels, body(): pl.pallas_call(finish, out_shape=(out, out), in_specs=[vmem, vmem], out_s...  1.68 us

profile of v3, /device:TPU:0, one launch (start us, length us, event | category | flops | bytes accessed | tf_op | source)
XLA Modules:
  0.0 73.2 jit_solution(5093643025620015297)
XLA Ops:
  1.9 69.6 %shard_map.158 = (f32[2,6,64,512]{3,2,1,0:T(8,128)S(1)}, f32[2,6,64,512]{3,2,1,0:T(8,128)S(1)}) custom-call(f32[2,6,64,512]{3,2,1,0:T(8,128)} %a_hbm.1, f32[2,6,64,512]{3,2,1,0:T(8,128)} %s_hbm.1, f32[2,64,512]{2,1,0:T(8,128)} %fs_hbm.1, f32[2,64,512]{2,1,0:T(8,128)} %fp_hbm.1, f32[2,64,512]{2,1,0:T(8,128)} %ds_hbm.1, f32[64,512]{1,0:T(8,128)} %vol_hbm.1, ...), custom_call_target="tpu_custom_call" | custom-call | tf_op jit(solution)/shard_map/pallas_call | solution.py:811
  71.6 1.7 %shard_map.159 = (f32[2,6,64,512]{3,2,1,0:T(8,128)}, f32[2,6,64,512]{3,2,1,0:T(8,128)}) custom-call(f32[2,6,64,512]{3,2,1,0:T(8,128)S(1)} %get-tuple-element.4.a, f32[2,6,64,512]{3,2,1,0:T(8,128)S(1)} %get-tuple-element.5.r), custom_call_target="tpu_custom_call" | custom-call | tf_op jit(solution)/shard_map/pallas_call | solution.py:866

commit v4 on v3

v4 whole, which is shorter than its diff:
```python
import functools
import math

import jax
import jax.numpy as jnp
from jax import lax
from jax.experimental import pallas as pl
from jax.experimental.pallas import tpu as pltpu
from jax.sharding import PartitionSpec as P

SWEEPS = 2
TILE = 8
LANES = 128
PARTS = 2
CHIP = 4
GROUP = 2
MESH = pl.DeviceIdType.MESH


def spectral_entry(offset, count):
    offset = offset % count
    if offset == 0 or 2 * offset == count:
        return 0.0
    return 0.5 * (-1.0) ** offset / math.tan(math.pi * offset / count)


def split_parts(value):
    parts = []
    for _ in range(PARTS):
        part = value.astype(jnp.bfloat16)
        parts.append(part)
        value = value - part.astype(jnp.float32)
    return parts


def kernel(
    n_space,
    n_inst,
    a_hbm,
    s_hbm,
    fs_hbm,
    fp_hbm,
    ds_hbm,
    vol_hbm,
    blocks_hbm,
    dinv_hbm,
    pblock_hbm,
    freq_hbm,
    shift_hbm,
    cells_hbm,
    targets_hbm,
    weights_hbm,
    counts_hbm,
    out_a,
    out_r,
    blocks,
    dinv,
    pblock,
    freq,
    shift,
    cells,
    targets,
    weights,
    counts,
    A,
    AT,
    ST,
    Y,
    RT,
    PT,
    NEAR,
    FAR,
    FS,
    FP,
    DS,
    VOL,
    DH,
    CL,
    CR,
    PW,
    PF,
    DV,
    DT,
    COL,
    PICK,
    ALLP,
    ROUTED,
    ARR,
    LHS,
    load_sem,
    own_r,
    in_s,
    in_r,
    c_s,
    c_r,
    r_s,
    r_r,
    cols_s,
    cols_r,
    hs,
    hr,
    ps,
    pr,
    q_s,
    q_r,
    token,
):
    per_dev, variables, rows, width = a_hbm.shape
    instances = n_inst * per_dev
    cols = width // 2
    slots = cells.shape[2]
    nb = rows // TILE
    part_rows = rows // 2
    inst = lax.axis_index("inst")
    me = lax.axis_index("space")
    odd = inst % 2
    sibling = inst + 1 - 2 * odd
    across = (inst + 2) % n_inst
    diagonal = (sibling + 2) % n_inst
    shift_bits = width.bit_length() - 1
    peers = (across, diagonal, sibling)
    mine = 2 * odd
    other = 2 - 2 * odd
    seats = (4 + mine, 4 + other, other)

    def remote(src, dst, send, recv, **device):
        return pltpu.make_async_remote_copy(
            src_ref=src, dst_ref=dst, send_sem=send, recv_sem=recv, device_id=device,
            device_id_type=MESH,
        )

    def half(c):
        return pl.ds(pl.multiple_of(c * cols, cols), cols)

    def pair(seat):
        return pl.ds(seat, per_dev)

    def local(src, dst, n):
        return pltpu.make_async_copy(src, dst, load_sem.at[n])

    inner = pl.ds(TILE, rows)
    here_cols = half(odd)
    loads = [
        local(a_hbm, A, 0),
        local(s_hbm.at[:, :, :, here_cols], ST.at[pair(mine)], 1),
        local(a_hbm.at[:, :, :, here_cols], AT.at[pair(mine), :, inner, :], 2),
        local(fp_hbm.at[:, :, here_cols], FP.at[pair(mine)], 3),
        local(fs_hbm.at[:, :, here_cols], FS.at[pair(mine), inner, :], 4),
        local(ds_hbm.at[:, :, here_cols], DS.at[pair(mine)], 5),
        local(vol_hbm.at[:, here_cols], VOL, 6),
        local(ds_hbm, DH, 7),
    ]
    tables = [
        local(dinv_hbm, dinv, 8),
        local(cells_hbm, cells, 9),
        local(counts_hbm, counts, 10),
        local(weights_hbm, weights, 11),
        local(pblock_hbm, pblock, 12),
        local(shift_hbm, shift, 13),
        local(targets_hbm, targets, 14),
        local(blocks_hbm, blocks, 15),
        local(freq_hbm, freq, 16),
    ]

    barrier = pltpu.get_barrier_semaphore()
    for peer in peers:
        pl.semaphore_signal(barrier, inc=1, device_id={"inst": peer}, device_id_type=MESH)

    has_hi = me < n_space - 2
    has_lo = me > 1
    hi = (me + 2) % n_space
    lo = (me + n_space - 2) % n_space
    partner = me + 1 - 2 * (me % 2)

    def greet(semaphore, device):
        pl.semaphore_signal(
            semaphore, inc=1, device_id={"space": device}, device_id_type=MESH
        )

    greet(barrier, partner)

    @pl.when(has_hi)
    def _():
        greet(barrier, hi)

    @pl.when(has_lo)
    def _():
        greet(barrier, lo)

    for copy in loads[:1] + tables + loads[1:]:
        copy.start()

    def incoming(n, target, seat):
        if n == 0:
            src, dst = a_hbm, AT.at[pair(seat), :, inner, :]
        else:
            src, dst = s_hbm, ST.at[pair(seat)]
        return remote(
            src.at[:, :, :, half(target)], dst, in_s.at[n], in_r.at[n], inst=sibling
        )

    def seat_there(kind):
        return mine + (4 if kind < 2 else 0)

    def target_half(kind):
        return odd if kind == 0 else 1 - odd

    def ds_copy(kind, column, seat):
        return remote(
            ds_hbm.at[:, :, half(column)], DS.at[pair(seat)],
            c_s.at[kind, 0], c_r.at[kind, 0], inst=peers[kind],
        )

    def fp_copy(kind, column, seat):
        return remote(
            fp_hbm.at[:, :, half(column)], FP.at[pair(seat)],
            c_s.at[kind, 1], c_r.at[kind, 1], inst=peers[kind],
        )

    def fs_part(part):
        def make(kind, column, seat):
            begin = part * part_rows
            return remote(
                fs_hbm.at[:, pl.ds(begin, part_rows), half(column)],
                FS.at[pair(seat), pl.ds(begin + TILE, part_rows), :],
                c_s.at[kind, 2 + part], c_r.at[kind, 2 + part], inst=peers[kind],
            )

        return make

    def dv_copy(kind, column, seat):
        return remote(
            DV.at[0], DV.at[kind + 1], c_s.at[kind, 4], c_r.at[kind, 4], inst=peers[kind]
        )

    fs_low, fs_high = fs_part(0), fs_part(1)
    linked, beside = (0, 1), (2,)

    def start(copy, kinds=(0, 1, 2)):
        for kind in kinds:
            copy(kind, target_half(kind), seat_there(kind)).start()

    def arrived(copy, kinds=(0, 1, 2)):
        for kind in kinds:
            copy(kind, odd, seats[kind]).wait_recv()

    def sent(copy, kinds=(0, 1, 2)):
        for kind in kinds:
            copy(kind, target_half(kind), seat_there(kind)).wait_send()

    def r_copy(kind, b, column):
        row = pl.multiple_of(b * TILE, TILE)
        land = FAR if kind < 2 else NEAR
        return remote(
            RT.at[pair(seats[kind]), :, pl.ds(row, TILE), :],
            land.at[:, :, pl.ds(row, TILE), half(column)],
            r_s.at[kind, b], r_r.at[kind, b], inst=peers[kind],
        )

    def r_own(b):
        row = pl.multiple_of(b * TILE, TILE)
        return pltpu.make_async_copy(
            RT.at[pair(mine), :, pl.ds(row, TILE), :],
            NEAR.at[:, :, pl.ds(row, TILE), here_cols], own_r.at[b],
        )

    has_above = me < n_space - 1
    has_below = me > 0
    above = (me + 1) % n_space
    below = (me + n_space - 1) % n_space
    field_of = (AT, Y.at[pl.ds(CHIP, CHIP)], Y.at[pl.ds(0, CHIP)])

    def halo_up(stage):
        ref = field_of[stage]
        return remote(
            ref.at[:, :, pl.ds(rows + TILE - 1, 1), :], ref.at[:, :, pl.ds(TILE - 1, 1), :],
            hs.at[2 * stage], hr.at[2 * stage], space=above,
        )

    def halo_down(stage):
        ref = field_of[stage]
        return remote(
            ref.at[:, :, pl.ds(TILE, 1), :], ref.at[:, :, pl.ds(rows + TILE, 1), :],
            hs.at[2 * stage + 1], hr.at[2 * stage + 1], space=below,
        )

    def halo_face(side):
        group = pl.ds(side * CHIP, CHIP)
        return remote(
            FS.at[group, pl.ds(rows + TILE - 1, 1), :], FS.at[group, pl.ds(TILE - 1, 1), :],
            hs.at[6 + side], hr.at[6 + side], space=above,
        )

    def col_right(stage):
        return remote(
            PW.at[stage], CL.at[stage], cols_s.at[stage], cols_r.at[stage], inst=sibling
        )

    def col_left(stage):
        return remote(
            PF.at[stage], CR.at[stage], cols_s.at[stage], cols_r.at[stage], inst=sibling
        )

    def halos_start(stage):
        @pl.when(has_above)
        def _():
            halo_up(stage).start()

        @pl.when(has_below)
        def _():
            halo_down(stage).start()

    def halos_wait(stage):
        @pl.when(has_below)
        def _():
            halo_up(stage).wait_recv()

        @pl.when(has_above)
        def _():
            halo_down(stage).wait_recv()

        @pl.when(odd == 1)
        def _():
            col_right(stage).wait_recv()

        @pl.when(odd == 0)
        def _():
            col_left(stage).wait_recv()

    def halos_sent(stage):
        @pl.when(has_above)
        def _():
            halo_up(stage).wait_send()

        @pl.when(has_below)
        def _():
            halo_down(stage).wait_send()

        @pl.when(odd == 0)
        def _():
            col_right(stage).wait_send()

        @pl.when(odd == 1)
        def _():
            col_left(stage).wait_send()

    def zeros(*shape):
        return jnp.zeros(shape, jnp.float32)

    @pl.when(me == 0)
    def _():
        FS[:, 0:TILE, :] = zeros(instances, TILE, cols)
        AT[:, :, 0:TILE, :] = zeros(CHIP, variables, TILE, cols)
        Y[:, :, 0:TILE, :] = zeros(instances, variables, TILE, cols)

    @pl.when(me == n_space - 1)
    def _():
        AT[:, :, rows + TILE : rows + 2 * TILE, :] = zeros(CHIP, variables, TILE, cols)
        Y[:, :, rows + TILE : rows + 2 * TILE, :] = zeros(instances, variables, TILE, cols)

    @pl.when(odd == 0)
    def _():
        CL[...] = zeros(3, rows, LANES)

    @pl.when(odd == 1)
    def _():
        CR[...] = zeros(3, rows, LANES)

    sub8 = lax.broadcasted_iota(jnp.int32, (TILE, cols), 0)
    lane8 = lax.broadcasted_iota(jnp.int32, (TILE, cols), 1)
    lane1 = lax.broadcasted_iota(jnp.int32, (TILE, LANES), 1)

    pl.semaphore_wait(barrier, n_inst + has_hi.astype(jnp.int32) + has_lo.astype(jnp.int32))

    start(ds_copy, linked)
    start(fp_copy, linked)
    incoming(0, 1 - odd, mine).start()
    start(fp_copy, beside)
    start(fs_high, beside)
    start(fs_low, beside)
    start(ds_copy, beside)
    incoming(1, 1 - odd, mine).start()

    tables[0].wait()
    packed = zeros(TILE, LANES)
    for k in range(per_dev):
        for u in range(variables):
            for v in range(variables):
                n = (k * variables + u) * variables + v
                packed = jnp.where(lane1 == n, dinv[u, k, v], packed)
    DV[0] = packed
    start(dv_copy)

    @pl.when(jnp.logical_not(has_hi))
    def _():
        greet(token.at[0], lo)

    @pl.when(jnp.logical_not(has_lo))
    def _():
        greet(token.at[1], hi)

    sub_w = lax.broadcasted_iota(jnp.int32, (width, slots), 0)
    sub_h = lax.broadcasted_iota(jnp.int32, (cols, slots), 0)
    sub_r = lax.broadcasted_iota(jnp.int32, (rows, slots), 0)

    def column_table(index, chunk):
        for q in range(TILE):
            line = index(chunk * TILE + q)
            column = jnp.bitwise_and(line, width - 1)
            hot = jnp.where(sub_w == column, 1.0, 0.0).astype(jnp.bfloat16)
            COL[:, q * slots : (q + 1) * slots] = hot

    def half_table(index, chunk):
        for q in range(TILE):
            line = index(chunk * TILE + q)
            column = jnp.bitwise_and(line, width - 1) - odd * cols
            hot = jnp.where(sub_h == column, 1.0, 0.0).astype(jnp.bfloat16)
            COL[0:cols, q * slots : (q + 1) * slots] = hot

    def cell_line(q):
        return cells[0, pl.ds(q, 1), :]

    def target_line(p):
        return targets[p, 0:1, :]

    chunks = n_space // TILE

    loads[0].wait()
    for copy in tables[1:]:
        copy.wait()

    @pl.loop(0, chunks)
    def _(chunk):
        column_table(cell_line, chunk)

        @pl.loop(0, per_dev)
        def _(k):
            field = A[k].reshape(variables * rows, width)
            stacked = jnp.concatenate(split_parts(field), axis=0)
            terms = jnp.dot(stacked, COL[...], preferred_element_type=jnp.float32)
            height = variables * rows
            found = terms[:height]
            for part in range(1, PARTS):
                found = found + terms[part * height : (part + 1) * height]
            for q in range(TILE):
                hit = sub_r == lax.shift_right_logical(cell_line(chunk * TILE + q), shift_bits)
                for v in range(variables):
                    piece = found[v * rows : (v + 1) * rows, q * slots : (q + 1) * slots]
                    PICK[k, v, chunk, q : q + 1, :] = jnp.sum(
                        jnp.where(hit, piece, 0.0), axis=0, keepdims=True
                    )

        lane = lax.broadcasted_iota(jnp.int32, (TILE, slots), 1)
        sub = lax.broadcasted_iota(jnp.int32, (TILE, slots), 0)
        limit = jnp.zeros((TILE, slots), jnp.int32)
        for q in range(TILE):
            limit = jnp.where(sub == q, counts[0, chunk * TILE + q], limit)
        first = pl.multiple_of(chunk * TILE, TILE)
        weight = jnp.where(lane < limit, weights[0, pl.ds(first, TILE), :], 0.0)

        for k in range(per_dev):
            picked = [PICK[k, v, chunk] for v in range(variables)]
            for u in range(variables):
                mixed = pblock[0, u] * picked[0]
                for v in range(1, variables):
                    mixed = mixed + pblock[v, u] * picked[v]
                ALLP[0, k, u, chunk] = mixed * weight

    p_x = remote(ALLP.at[0], ALLP.at[2], ps.at[0], pr.at[0], inst=across)
    p_sib = remote(ALLP.at[0], ALLP.at[3 - 2 * odd], ps.at[1], pr.at[1 + odd], inst=sibling)
    p_rel = remote(ALLP.at[2], ALLP.at[1 + 2 * odd], ps.at[2], pr.at[2 - odd], inst=sibling)
    p_sib_in = remote(ALLP.at[0], ALLP.at[1 + 2 * odd], ps.at[1], pr.at[2 - odd], inst=sibling)
    p_rel_in = remote(ALLP.at[2], ALLP.at[3 - 2 * odd], ps.at[2], pr.at[1 + odd], inst=sibling)
    p_x.start()
    p_sib.start()
    start(fs_high, linked)
    start(fs_low, linked)

    @pl.when(has_hi)
    def _():
        pl.semaphore_wait(token.at[0], 1)

        @pl.when(has_lo)
        def _():
            greet(token.at[0], lo)

    @pl.when(has_lo)
    def _():
        pl.semaphore_wait(token.at[1], 1)

        @pl.when(has_hi)
        def _():
            greet(token.at[1], hi)

    for copy in loads[1:]:
        copy.wait()
    for n in range(2):
        incoming(n, odd, other).wait_recv()
    for copy in (fp_copy, fs_high, fs_low):
        arrived(copy, beside)
    halos_start(0)

    @pl.when(has_above)
    def _():
        halo_face(0).start()

    def wide(tile):
        return jnp.concatenate([tile] * (cols // LANES), axis=1)

    def pack(stage, ref, base):
        @pl.loop(0, nb)
        def _(b):
            row = pl.multiple_of(b * TILE, TILE)
            here = pl.ds(row, TILE)
            mid = pl.ds(row + TILE, TILE)
            last = zeros(TILE, LANES)
            first = zeros(TILE, LANES)
            for r in range(CHIP):
                fp = FP[base + r, here, cols - LANES : cols]
                for v in range(variables):
                    n = r * variables + v
                    a = ref[base + r, v, mid, 0:LANES]
                    w = fp * ref[base + r, v, mid, cols - LANES : cols]
                    first = jnp.where(lane1 == n, pltpu.roll(a, n, 1) if n else a, first)
                    last = jnp.where(lane1 == n, pltpu.roll(w, n + 1, 1), last)
            PW[stage, here, :] = last
            PF[stage, here, :] = first

        @pl.when(odd == 0)
        def _():
            col_right(stage).start()

        @pl.when(odd == 1)
        def _():
            col_left(stage).start()

    pack(0, AT, 0)

    arrived(dv_copy)
    for position in range(instances):
        if position < CHIP:
            kind = jnp.where(odd == position // per_dev, 0, 3)
        else:
            kind = jnp.where(odd == (position - CHIP) // per_dev, 1, 2)
        vector = DV[kind]
        for n in range(variables * variables):
            lane = (position % per_dev) * variables * variables + n
            DT[position * variables * variables + n] = jnp.broadcast_to(
                vector[:, lane : lane + 1], (TILE, LANES)
            )

    arrived(ds_copy)

    f1, f2, f3 = (spectral_entry(d, instances) for d in (1, 2, 3))

    def spectral(a, row):
        here = pl.ds(row, TILE)
        scaled = freq[0] * VOL[here, :]
        v1 = (0.5 * (f1 - f3)) * scaled
        v2 = f2 * scaled
        v3 = (0.5 * (f1 + f3)) * scaled
        results = []
        for u in range(variables):
            near = [a(r, u) for r in range(4)]
            far = [a(r, u) for r in range(4, 8)]
            b = [m if f is None else m - f for m, f in zip(near, far)]
            c = [m if f is None else m + f for m, f in zip(near, far)]
            even = v1 * (c[1] - c[3])
            odds = v1 * (c[2] - c[0])
            q = [even, odds, -even, -odds]
            p = [
                v2 * b[2] + v3 * (b[1] + b[3]),
                v2 * b[3] + v3 * (b[2] - b[0]),
                v3 * (b[3] - b[1]) - v2 * b[0],
                -(v2 * b[1] + v3 * (b[0] + b[2])),
            ]
            results.append((q, p))
        return results

    def coupling(acc, span, ref, row, stage):
        here = pl.ds(row, TILE)
        mid = pl.ds(row + TILE, TILE)
        low = pl.ds(row, TILE)
        high = pl.ds(row + 2 * TILE, TILE)
        top = sub8 == TILE - 1
        bottom = sub8 == 0
        fm = {r: FS[r, mid, :] for r in span}
        fl = {r: jnp.where(top, FS[r, low, :], fm[r]) for r in span}
        fp = {r: FP[r, here, :] for r in span}
        cl = CL[stage, here, :]
        cr = CR[stage, here, :]
        for v in range(variables):
            terms = {}
            for r in span:
                n = (r % CHIP) * variables + v
                a = ref[r, v, mid, :]
                x = pltpu.roll(fl[r] * jnp.where(top, ref[r, v, low, :], a), 1, 0)
                y = fm[r] * pltpu.roll(
                    jnp.where(bottom, ref[r, v, high, :], a), TILE - 1, 0
                )
                edge = wide(pltpu.roll(cl, LANES - n, 1) if n else cl)
                left = jnp.where(lane8 == 0, edge, pltpu.roll(fp[r] * a, 1, 1))
                edge = wide(pltpu.roll(cr, LANES - 1 - n, 1))
                right = fp[r] * jnp.where(
                    lane8 == cols - 1, edge, pltpu.roll(a, cols - 1, 1)
                )
                terms[r] = (x, y, left, right)
            for u in range(variables):
                k0, k1, k2, k3 = (blocks[v, n, u] for n in range(4))
                for r in span:
                    x, y, left, right = terms[r]
                    acc[r, u] = acc[r, u] - ((k0 * x + k1 * y) + (k2 * left + k3 * right))
        return acc

    def inverse(acc, r, u, here):
        n = (r * variables + u) * variables
        new = wide(DT[n]) * acc[0]
        for v in range(1, variables):
            new = new + wide(DT[n + v]) * acc[v]
        return DS[r, here, :] * new

    halos_wait(0)

    @pl.when(has_below)
    def _():
        halo_face(0).wait_recv()

    @pl.loop(0, nb)
    def _(b):
        row = pl.multiple_of(b * TILE, TILE)
        here = pl.ds(row, TILE)
        mid = pl.ds(row + TILE, TILE)
        found = spectral(lambda r, u: AT[r, u, mid, :] if r < CHIP else None, row)
        for u, (q, p) in enumerate(found):
            for r in range(CHIP):
                RT[r, u, here, :] = ST[r, u, here, :] - (q[r] + p[r])
                RT[CHIP + r, u, here, :] = p[r] - q[r]
        for base in range(0, instances, GROUP):
            span = range(base, base + GROUP)
            acc = {(r, u): RT[r, u, here, :] for r in span for u in range(variables)}
            if base < CHIP:
                acc = coupling(acc, span, AT, row, 0)
            for r in span:
                line = [acc[r, v] for v in range(variables)]
                for u in range(variables):
                    Y[r, u, mid, :] = inverse(line, r, u, here)

    halos_start(1)
    arrived(fp_copy, linked)
    pack(1, Y, CHIP)

    p_x.wait_recv()
    p_rel.start()
    p_sib_in.wait_recv()
    p_rel_in.wait_recv()

    @pl.loop(0, instances)
    def _(k):
        wanted = lax.rem(k - shift[0] + 2 * instances, instances)
        group = lax.div(wanted, per_dev)
        member = lax.rem(wanted, per_dev)

        @pl.loop(0, chunks)
        def _(chunk):
            for u in range(variables):
                value = ALLP[group, member, u, chunk]
                for q in range(TILE):
                    ROUTED[chunk * TILE + q, k, u : u + 1, :] = value[q : q + 1, :]

    def a2a(j):
        return remote(
            ROUTED.at[(me + j) % n_space], ARR.at[me], q_s.at[j], q_r.at[j],
            space=(me + j) % n_space,
        )

    @pl.loop(1, n_space)
    def _(j):
        a2a(j).start()

    ARR[me] = ROUTED[me]
    halos_wait(1)
    arrived(fs_high, linked)

    @pl.when(has_above)
    def _():
        halo_face(1).start()

    def order(n):
        return (n + nb // 2 + 1) % nb

    @pl.loop(0, nb)
    def _(t):
        @pl.when(t == nb // 2 - 1)
        def _():
            arrived(fs_low, linked)

            @pl.when(has_below)
            def _():
                halo_face(1).wait_recv()

        b = order(t)
        row = pl.multiple_of(b * TILE, TILE)
        here = pl.ds(row, TILE)
        mid = pl.ds(row + TILE, TILE)
        found = spectral(lambda r, u: Y[r, u, mid, :], row)
        for u, (q, p) in enumerate(found):
            for r in range(CHIP):
                RT[CHIP + r, u, here, :] = p[r] - q[r]
        for base in range(CHIP, instances, GROUP):
            span = range(base, base + GROUP)
            acc = {(r, u): RT[r, u, here, :] for r in span for u in range(variables)}
            acc = coupling(acc, span, Y, row, 1)
            for r in span:
                for u in range(variables):
                    RT[r, u, here, :] = acc[r, u]
        r_copy(0, b, odd).start()
        r_copy(1, b, odd).start()

    half_table(target_line, 0)

    @pl.loop(1, n_space)
    def _(j):
        remote(
            ROUTED.at[0], ARR.at[(me + n_space - j) % n_space], q_s.at[j], q_r.at[j],
            space=(me + j) % n_space,
        ).wait_recv()

    if chunks > 1:
        PT[...] = zeros(instances, variables, rows, cols)

    @pl.loop(0, chunks)
    def _(chunk):
        if chunks > 1:
            half_table(target_line, chunk)

        @pl.loop(0, instances)
        def _(r):
            k = (r + instances - mine) % instances
            for p in range(TILE):
                hit = sub_r == lax.shift_right_logical(target_line(chunk * TILE + p), shift_bits)
                parts = split_parts(ARR[chunk * TILE + p, k])
                for n, part in enumerate(parts):
                    for u in range(variables):
                        begin = (n * variables + u) * rows
                        LHS[begin : begin + rows, p * slots : (p + 1) * slots] = jnp.where(
                            hit, part[u : u + 1, :].astype(jnp.float32), 0.0
                        ).astype(jnp.bfloat16)
            terms = lax.dot_general(
                LHS[...], COL[0:cols, :], (((1,), (1,)), ((), ())),
                preferred_element_type=jnp.float32,
            )
            height = variables * rows
            summed = terms[:height]
            for part in range(1, PARTS):
                summed = summed + terms[part * height : (part + 1) * height]
            summed = summed.reshape(variables, rows, cols)
            if chunks > 1:
                summed = summed + PT[r]
            PT[r] = summed

    halos_sent(1)

    @pl.loop(0, nb)
    def _(b):
        row = pl.multiple_of(b * TILE, TILE)
        here = pl.ds(row, TILE)
        mid = pl.ds(row + TILE, TILE)
        for r in range(instances):
            line = [PT[r, v, here, :] for v in range(variables)]
            for u in range(variables):
                Y[r, u, mid, :] = Y[r, u, mid, :] - inverse(line, r, u, here)
                if r < CHIP:
                    ST[r, u, here, :] = ST[r, u, here, :] - line[u]

    halos_start(2)
    pack(2, Y, 0)
    halos_wait(2)

    @pl.loop(0, nb)
    def _(b):
        row = pl.multiple_of(b * TILE, TILE)
        here = pl.ds(row, TILE)
        mid = pl.ds(row + TILE, TILE)
        found = spectral(lambda r, u: Y[r, u, mid, :], row)
        for u, (q, p) in enumerate(found):
            for r in range(CHIP):
                RT[r, u, here, :] = ST[r, u, here, :] - (q[r] + p[r])
        for base in range(0, CHIP, GROUP):
            span = range(base, base + GROUP)
            acc = {(r, u): RT[r, u, here, :] for r in span for u in range(variables)}
            acc = coupling(acc, span, Y, row, 2)
            for r in span:
                for u in range(variables):
                    RT[r, u, here, :] = acc[r, u]
        r_copy(2, b, odd).start()
        r_own(b).start()

    @pl.loop(0, nb)
    def _(t):
        b = order(t)
        here = pl.ds(pl.multiple_of(b * TILE, TILE), TILE)
        r_own(b).wait()
        r_copy(2, b, 1 - odd).wait_recv()
        r_copy(0, b, odd).wait_recv()
        r_copy(1, b, 1 - odd).wait_recv()
        for k in range(per_dev):
            scale = DH[k, here, :]
            rest = [NEAR[k, v, here, :] + FAR[k, v, here, :] for v in range(variables)]
            for u in range(variables):
                out_r[k, u, here, :] = rest[u]
                new = dinv[u, k, 0] * rest[0]
                for v in range(1, variables):
                    new = new + dinv[u, k, v] * rest[v]
                out_a[k, u, here, :] = scale * new

    for copy in (ds_copy, dv_copy, fp_copy, fs_low, fs_high):
        sent(copy)
    for n in range(2):
        incoming(n, 1 - odd, mine).wait_send()

    p_x.wait_send()
    p_sib.wait_send()
    p_rel.wait_send()

    @pl.loop(1, n_space)
    def _(j):
        a2a(j).wait_send()

    @pl.when(has_above)
    def _():
        halo_face(0).wait_send()
        halo_face(1).wait_send()

    halos_sent(0)
    halos_sent(2)

    @pl.loop(0, nb)
    def _(b):
        for kind in range(3):
            r_copy(kind, b, odd).wait_send()


def finish(a, r, out_a, out_r, sems):
    copies = [
        pltpu.make_async_copy(a, out_a, sems.at[0]),
        pltpu.make_async_copy(r, out_r, sems.at[1]),
    ]
    for copy in copies:
        copy.start()
    for copy in copies:
        copy.wait()


def body(n_space, n_inst, a, s, fs, fp, ds, vol, blocks, dinv, *rest):
    per_dev, variables, rows, width = a.shape
    slots = rest[3].shape[2]
    nb = rows // TILE
    chunks = n_space // TILE
    instances = n_inst * per_dev
    cols = width // 2
    f32 = jnp.float32
    hbm = pl.BlockSpec(memory_space=pl.ANY)
    vmem = pl.BlockSpec(memory_space=pltpu.VMEM)
    dma = pltpu.SemaphoreType.DMA
    field = (per_dev, variables, rows, width)
    out = jax.ShapeDtypeStruct(field, f32)
    blocks = jnp.transpose(blocks, (1, 0, 2))
    dinv = jnp.transpose(dinv, (1, 0, 2))
    placed = pltpu.VMEM(field, f32)
    new, r = pl.pallas_call(
        functools.partial(kernel, n_space, n_inst),
        out_shape=(placed, placed),
        in_specs=[hbm] * 15,
        out_specs=(vmem, vmem),
        scratch_shapes=[
            pltpu.SMEM(blocks.shape, f32),
            pltpu.SMEM(dinv.shape, f32),
            pltpu.SMEM(rest[0].shape, f32),
            pltpu.SMEM(rest[1].shape, f32),
            pltpu.SMEM(rest[2].shape, jnp.int32),
            pltpu.VMEM(rest[3].shape, jnp.int32),
            pltpu.VMEM(rest[4].shape, jnp.int32),
            pltpu.VMEM(rest[5].shape, f32),
            pltpu.SMEM(rest[6].shape, jnp.int32),
            pltpu.VMEM(field, f32),
            pltpu.VMEM((CHIP, variables, rows + 2 * TILE, cols), f32),
            pltpu.VMEM((CHIP, variables, rows, cols), f32),
            pltpu.VMEM((instances, variables, rows + 2 * TILE, cols), f32),
            pltpu.VMEM((instances, variables, rows, cols), f32),
            pltpu.VMEM((instances, variables, rows, cols), f32),
            pltpu.VMEM(field, f32),
            pltpu.VMEM(field, f32),
            pltpu.VMEM((instances, rows + TILE, cols), f32),
            pltpu.VMEM((instances, rows, cols), f32),
            pltpu.VMEM((instances, rows, cols), f32),
            pltpu.VMEM((rows, cols), f32),
            pltpu.VMEM((per_dev, rows, width), f32),
            pltpu.VMEM((3, rows, LANES), f32),
            pltpu.VMEM((3, rows, LANES), f32),
            pltpu.VMEM((3, rows, LANES), f32),
            pltpu.VMEM((3, rows, LANES), f32),
            pltpu.VMEM((n_inst, TILE, LANES), f32),
            pltpu.VMEM((instances * variables * variables, TILE, LANES), f32),
            pltpu.VMEM((width, TILE * slots), jnp.bfloat16),
            pltpu.VMEM((per_dev, variables, chunks, TILE, slots), f32),
            pltpu.VMEM((4, per_dev, variables, chunks, TILE, slots), f32),
            pltpu.VMEM((n_space, instances, variables, slots), f32),
            pltpu.VMEM((n_space, instances, variables, slots), f32),
            pltpu.VMEM((PARTS * variables * rows, TILE * slots), jnp.bfloat16),
            dma((17,)),
            dma((nb,)),
            dma((2,)),
            dma((2,)),
            dma((3, 5)),
            dma((3, 5)),
            dma((3, nb)),
            dma((3, nb)),
            dma((3,)),
            dma((3,)),
            dma((8,)),
            dma((8,)),
            dma((3,)),
            dma((3,)),
            dma((n_space,)),
            dma((n_space,)),
            pltpu.SemaphoreType.REGULAR((2,)),
        ],
        compiler_params=pltpu.CompilerParams(
            collective_id=0, has_side_effects=True, vmem_limit_bytes=56 * 1024 * 1024
        ),
    )(a, s, fs, fp, ds, vol, blocks, dinv, *rest)
    return pl.pallas_call(
        finish,
        out_shape=(out, out),
        in_specs=[vmem, vmem],
        out_specs=(hbm, hbm),
        scratch_shapes=[dma((2,))],
    )(*(pltpu.with_memory_space_constraint(x, pltpu.VMEM) for x in (new, r)))


def solution(mesh):
    in_specs = (
        P("inst", None, "space", None),
        P("inst", None, "space", None),
        P("inst", "space", None),
        P("inst", "space", None),
        P("inst", "space", None),
        P("space", None),
        P(),
        P("inst", None, None),
        P(),
        P(),
        P(),
        P("space", None, None),
        P(None, "space", None),
        P("space", None, None),
        P("space", None),
    )
    out_specs = (P("inst", None, "space", None), P("inst", None, "space", None))
    return jax.shard_map(
        functools.partial(body, mesh.shape["space"], mesh.shape["inst"]),
        mesh=mesh,
        in_specs=in_specs,
        out_specs=out_specs,
        check_vma=False,
    )
```

time: 73.4 us -> 67.1 us (0.914)
  Pallas kernels: 71.3 us -> 64.6 us
    pallas_call x1, Pallas kernels: 69.6 us -> 62.9 us  [body(): pl.pallas_call(functools.partial(kernel, n_space, n_inst), out_shape=(pla...]
where the time goes in v4:
time: 67.1 us; the launch traced here: 66.5 us
  Pallas kernels  64.6 us (96%)
  between operations  1.93 us (3%)
    pallas_call x1, Pallas kernels, body(): pl.pallas_call(functools.partial(kernel, n_space, n_inst), out_shape=(pla...  62.9 us
    pallas_call x1, Pallas kernels, body(): pl.pallas_call(finish, out_shape=(out, out), in_specs=[vmem, vmem], out_s...  1.68 us

profile of v4, /device:TPU:0, one launch (start us, length us, event | category | flops | bytes accessed | tf_op | source)
XLA Modules:
  0.0 66.5 jit_solution(7848826733286710145)
XLA Ops:
  1.9 62.9 %shard_map.158 = (f32[2,6,64,512]{3,2,1,0:T(8,128)S(1)}, f32[2,6,64,512]{3,2,1,0:T(8,128)S(1)}) custom-call(f32[2,6,64,512]{3,2,1,0:T(8,128)} %a_hbm.1, f32[2,6,64,512]{3,2,1,0:T(8,128)} %s_hbm.1, f32[2,64,512]{2,1,0:T(8,128)} %fs_hbm.1, f32[2,64,512]{2,1,0:T(8,128)} %fp_hbm.1, f32[2,64,512]{2,1,0:T(8,128)} %ds_hbm.1, f32[64,512]{1,0:T(8,128)} %vol_hbm.1, ...), custom_call_target="tpu_custom_call" | custom-call | tf_op jit(solution)/shard_map/pallas_call | solution.py:870
  64.9 1.7 %shard_map.159 = (f32[2,6,64,512]{3,2,1,0:T(8,128)}, f32[2,6,64,512]{3,2,1,0:T(8,128)}) custom-call(f32[2,6,64,512]{3,2,1,0:T(8,128)S(1)} %get-tuple-element.4.a, f32[2,6,64,512]{3,2,1,0:T(8,128)S(1)} %get-tuple-element.5.r), custom_call_target="tpu_custom_call" | custom-call | tf_op jit(solution)/shard_map/pallas_call | solution.py:932

commit v5 on v4

--- a/solution.py
+++ b/solution.py
@@ -205,35 +205,30 @@
     def target_half(kind):
         return odd if kind == 0 else 1 - odd
 
-    def ds_copy(kind, column, seat):
-        return remote(
-            ds_hbm.at[:, :, half(column)], DS.at[pair(seat)],
-            c_s.at[kind, 0], c_r.at[kind, 0], inst=peers[kind],
-        )
-
-    def fp_copy(kind, column, seat):
-        return remote(
-            fp_hbm.at[:, :, half(column)], FP.at[pair(seat)],
-            c_s.at[kind, 1], c_r.at[kind, 1], inst=peers[kind],
-        )
-
-    def fs_part(part):
+    def share(which, part):
+        begin = part * part_rows
+        span = pl.ds(begin, part_rows)
+        src, dst, land = (
+            (ds_hbm, DS, span),
+            (fp_hbm, FP, span),
+            (fs_hbm, FS, pl.ds(begin + TILE, part_rows)),
+        )[which]
+        n = 2 * which + part
+
         def make(kind, column, seat):
-            begin = part * part_rows
             return remote(
-                fs_hbm.at[:, pl.ds(begin, part_rows), half(column)],
-                FS.at[pair(seat), pl.ds(begin + TILE, part_rows), :],
-                c_s.at[kind, 2 + part], c_r.at[kind, 2 + part], inst=peers[kind],
+                src.at[:, span, half(column)], dst.at[pair(seat), land, :],
+                c_s.at[kind, n], c_r.at[kind, n], inst=peers[kind],
             )
 
         return make
 
     def dv_copy(kind, column, seat):
         return remote(
-            DV.at[0], DV.at[kind + 1], c_s.at[kind, 4], c_r.at[kind, 4], inst=peers[kind]
-        )
-
-    fs_low, fs_high = fs_part(0), fs_part(1)
+            DV.at[0], DV.at[kind + 1], c_s.at[kind, 6], c_r.at[kind, 6], inst=peers[kind]
+        )
+
+    lower, upper = ([share(which, part) for which in range(3)] for part in range(2))
     linked, beside = (0, 1), (2,)
 
     def start(copy, kinds=(0, 1, 2)):
@@ -291,58 +286,50 @@
             hs.at[6 + side], hr.at[6 + side], space=above,
         )
 
-    def col_right(stage):
-        return remote(
-            PW.at[stage], CL.at[stage], cols_s.at[stage], cols_r.at[stage], inst=sibling
-        )
-
-    def col_left(stage):
-        return remote(
-            PF.at[stage], CR.at[stage], cols_s.at[stage], cols_r.at[stage], inst=sibling
-        )
-
-    def halos_start(stage):
-        @pl.when(has_above)
-        def _():
-            halo_up(stage).start()
-
-        @pl.when(has_below)
-        def _():
-            halo_down(stage).start()
-
-    def halos_wait(stage):
-        @pl.when(has_below)
-        def _():
-            halo_up(stage).wait_recv()
-
-        @pl.when(has_above)
-        def _():
-            halo_down(stage).wait_recv()
-
-        @pl.when(odd == 1)
-        def _():
-            col_right(stage).wait_recv()
-
-        @pl.when(odd == 0)
-        def _():
-            col_left(stage).wait_recv()
-
-    def halos_sent(stage):
-        @pl.when(has_above)
-        def _():
-            halo_up(stage).wait_send()
-
-        @pl.when(has_below)
-        def _():
-            halo_down(stage).wait_send()
-
-        @pl.when(odd == 0)
-        def _():
-            col_right(stage).wait_send()
-
-        @pl.when(odd == 1)
-        def _():
-            col_left(stage).wait_send()
+    def col_copies(stage, span, n):
+        return (
+            remote(
+                PW.at[stage, span], CL.at[stage, span], cols_s.at[n], cols_r.at[n], inst=sibling
+            ),
+            remote(
+                PF.at[stage, span], CR.at[stage, span], cols_s.at[n], cols_r.at[n], inst=sibling
+            ),
+        )
+
+    def col_do(way, stage, span, n):
+        to_right, to_left = col_copies(stage, span, n)
+        is_left = odd == 0
+        if way == "receive":
+            is_left = odd == 1
+
+        @pl.when(is_left)
+        def _():
+            act(way, to_right)
+
+        @pl.when(jnp.logical_not(is_left))
+        def _():
+            act(way, to_left)
+
+    def act(way, copy):
+        if way == "start":
+            copy.start()
+        elif way == "receive":
+            copy.wait_recv()
+        else:
+            copy.wait_send()
+
+    def rows_do(way, stage):
+        up, down = has_above, has_below
+        if way == "receive":
+            up, down = has_below, has_above
+
+        @pl.when(up)
+        def _():
+            act(way, halo_up(stage))
+
+        @pl.when(down)
+        def _():
+            act(way, halo_down(stage))
 
     def zeros(*shape):
         return jnp.zeros(shape, jnp.float32)
@@ -372,13 +359,11 @@
 
     pl.semaphore_wait(barrier, n_inst + has_hi.astype(jnp.int32) + has_lo.astype(jnp.int32))
 
-    start(ds_copy, linked)
-    start(fp_copy, linked)
+    for copy in upper:
+        start(copy, linked)
     incoming(0, 1 - odd, mine).start()
-    start(fp_copy, beside)
-    start(fs_high, beside)
-    start(fs_low, beside)
-    start(ds_copy, beside)
+    for copy in upper + lower:
+        start(copy, beside)
     incoming(1, 1 - odd, mine).start()
 
     tables[0].wait()
@@ -473,8 +458,8 @@
     p_rel_in = remote(ALLP.at[2], ALLP.at[3 - 2 * odd], ps.at[2], pr.at[1 + odd], inst=sibling)
     p_x.start()
     p_sib.start()
-    start(fs_high, linked)
-    start(fs_low, linked)
+    for copy in lower:
+        start(copy, linked)
 
     @pl.when(has_hi)
     def _():
@@ -496,9 +481,9 @@
         copy.wait()
     for n in range(2):
         incoming(n, odd, other).wait_recv()
-    for copy in (fp_copy, fs_high, fs_low):
+    for copy in upper + lower:
         arrived(copy, beside)
-    halos_start(0)
+    rows_do("start", 0)
 
     @pl.when(has_above)
     def _():
@@ -507,34 +492,29 @@
     def wide(tile):
         return jnp.concatenate([tile] * (cols // LANES), axis=1)
 
-    def pack(stage, ref, base):
-        @pl.loop(0, nb)
-        def _(b):
-            row = pl.multiple_of(b * TILE, TILE)
-            here = pl.ds(row, TILE)
-            mid = pl.ds(row + TILE, TILE)
-            last = zeros(TILE, LANES)
-            first = zeros(TILE, LANES)
-            for r in range(CHIP):
-                fp = FP[base + r, here, cols - LANES : cols]
-                for v in range(variables):
-                    n = r * variables + v
-                    a = ref[base + r, v, mid, 0:LANES]
-                    w = fp * ref[base + r, v, mid, cols - LANES : cols]
-                    first = jnp.where(lane1 == n, pltpu.roll(a, n, 1) if n else a, first)
-                    last = jnp.where(lane1 == n, pltpu.roll(w, n + 1, 1), last)
-            PW[stage, here, :] = last
-            PF[stage, here, :] = first
-
-        @pl.when(odd == 0)
-        def _():
-            col_right(stage).start()
-
-        @pl.when(odd == 1)
-        def _():
-            col_left(stage).start()
-
-    pack(0, AT, 0)
+    whole = pl.ds(0, rows)
+
+    def pack(stage, ref, base, row):
+        here = pl.ds(row, TILE)
+        mid = pl.ds(row + TILE, TILE)
+        last = zeros(TILE, LANES)
+        first = zeros(TILE, LANES)
+        for r in range(CHIP):
+            fp = FP[base + r, here, cols - LANES : cols]
+            for v in range(variables):
+                n = r * variables + v
+                a = ref[base + r, v, mid, 0:LANES]
+                w = fp * ref[base + r, v, mid, cols - LANES : cols]
+                first = jnp.where(lane1 == n, pltpu.roll(a, n, 1) if n else a, first)
+                last = jnp.where(lane1 == n, pltpu.roll(w, n + 1, 1), last)
+        PW[stage, here, :] = last
+        PF[stage, here, :] = first
+
+    @pl.loop(0, nb)
+    def _(b):
+        pack(0, AT, 0, pl.multiple_of(b * TILE, TILE))
+
+    col_do("start", 0, whole, nb)
 
     arrived(dv_copy)
     for position in range(instances):
@@ -549,7 +529,12 @@
                 vector[:, lane : lane + 1], (TILE, LANES)
             )
 
-    arrived(ds_copy)
+    for copy in upper:
+        arrived(copy, linked)
+
+    @pl.when(has_above)
+    def _():
+        halo_face(1).start()
 
     f1, f2, f3 = (spectral_entry(d, instances) for d in (1, 2, 3))
 
@@ -619,14 +604,16 @@
             new = new + wide(DT[n + v]) * acc[v]
         return DS[r, here, :] * new
 
-    halos_wait(0)
+    rows_do("receive", 0)
+    col_do("receive", 0, whole, nb)
 
     @pl.when(has_below)
     def _():
         halo_face(0).wait_recv()
 
-    @pl.loop(0, nb)
-    def _(b):
+    middle = nb // 2
+
+    def sweep(b):
         row = pl.multiple_of(b * TILE, TILE)
         here = pl.ds(row, TILE)
         mid = pl.ds(row + TILE, TILE)
@@ -644,64 +631,14 @@
                 line = [acc[r, v] for v in range(variables)]
                 for u in range(variables):
                     Y[r, u, mid, :] = inverse(line, r, u, here)
-
-    halos_start(1)
-    arrived(fp_copy, linked)
-    pack(1, Y, CHIP)
-
-    p_x.wait_recv()
-    p_rel.start()
-    p_sib_in.wait_recv()
-    p_rel_in.wait_recv()
-
-    @pl.loop(0, instances)
-    def _(k):
-        wanted = lax.rem(k - shift[0] + 2 * instances, instances)
-        group = lax.div(wanted, per_dev)
-        member = lax.rem(wanted, per_dev)
-
-        @pl.loop(0, chunks)
-        def _(chunk):
-            for u in range(variables):
-                value = ALLP[group, member, u, chunk]
-                for q in range(TILE):
-                    ROUTED[chunk * TILE + q, k, u : u + 1, :] = value[q : q + 1, :]
-
-    def a2a(j):
-        return remote(
-            ROUTED.at[(me + j) % n_space], ARR.at[me], q_s.at[j], q_r.at[j],
-            space=(me + j) % n_space,
-        )
-
-    @pl.loop(1, n_space)
-    def _(j):
-        a2a(j).start()
-
-    ARR[me] = ROUTED[me]
-    halos_wait(1)
-    arrived(fs_high, linked)
-
-    @pl.when(has_above)
-    def _():
-        halo_face(1).start()
-
-    def order(n):
-        return (n + nb // 2 + 1) % nb
-
-    @pl.loop(0, nb)
-    def _(t):
-        @pl.when(t == nb // 2 - 1)
-        def _():
-            arrived(fs_low, linked)
-
-            @pl.when(has_below)
-            def _():
-                halo_face(1).wait_recv()
-
-        b = order(t)
+        pack(1, Y, CHIP, row)
+        col_do("start", 1, here, b)
+
+    def export(b):
         row = pl.multiple_of(b * TILE, TILE)
         here = pl.ds(row, TILE)
         mid = pl.ds(row + TILE, TILE)
+        col_do("receive", 1, here, b)
         found = spectral(lambda r, u: Y[r, u, mid, :], row)
         for u, (q, p) in enumerate(found):
             for r in range(CHIP):
@@ -715,6 +652,77 @@
                     RT[r, u, here, :] = acc[r, u]
         r_copy(0, b, odd).start()
         r_copy(1, b, odd).start()
+
+    def order(t):
+        early = (t < middle - 2).astype(jnp.int32)
+        late = (t >= nb - 2).astype(jnp.int32)
+        between = (1 - early) * (1 - late)
+        return (
+            early * (t + middle + 1)
+            + between * (t - middle + 3)
+            + late * (nb - 1 - t) * (nb - 1)
+        )
+
+    @pl.loop(0, nb + 4)
+    def _(n):
+        @pl.when(n < nb)
+        def _():
+            @pl.when(n == middle)
+            def _():
+                for copy in lower:
+                    arrived(copy, linked)
+
+            sweep((n + middle) % nb)
+
+        @pl.when(n == middle)
+        def _():
+            rows_do("start", 1)
+
+        @pl.when(n == nb + 2)
+        def _():
+            rows_do("receive", 1)
+
+            @pl.when(has_below)
+            def _():
+                halo_face(1).wait_recv()
+
+        @pl.when((n >= 2) & (n < middle))
+        def _():
+            export(order(n - 2))
+
+        @pl.when(n >= middle + 2)
+        def _():
+            export(order(n - 4))
+
+    p_x.wait_recv()
+    p_rel.start()
+    p_sib_in.wait_recv()
+    p_rel_in.wait_recv()
+
+    @pl.loop(0, instances)
+    def _(k):
+        wanted = lax.rem(k - shift[0] + 2 * instances, instances)
+        group = lax.div(wanted, per_dev)
+        member = lax.rem(wanted, per_dev)
+
+        @pl.loop(0, chunks)
+        def _(chunk):
+            for u in range(variables):
+                value = ALLP[group, member, u, chunk]
+                for q in range(TILE):
+                    ROUTED[chunk * TILE + q, k, u : u + 1, :] = value[q : q + 1, :]
+
+    def a2a(j):
+        return remote(
+            ROUTED.at[(me + j) % n_space], ARR.at[me], q_s.at[j], q_r.at[j],
+            space=(me + j) % n_space,
+        )
+
+    @pl.loop(1, n_space)
+    def _(j):
+        a2a(j).start()
+
+    ARR[me] = ROUTED[me]
 
     half_table(target_line, 0)
 
@@ -758,7 +766,7 @@
                 summed = summed + PT[r]
             PT[r] = summed
 
-    halos_sent(1)
+    rows_do("sent", 1)
 
     @pl.loop(0, nb)
     def _(b):
@@ -772,9 +780,15 @@
                 if r < CHIP:
                     ST[r, u, here, :] = ST[r, u, here, :] - line[u]
 
-    halos_start(2)
-    pack(2, Y, 0)
-    halos_wait(2)
+    rows_do("start", 2)
+
+    @pl.loop(0, nb)
+    def _(b):
+        pack(2, Y, 0, pl.multiple_of(b * TILE, TILE))
+
+    col_do("start", 2, whole, nb + 1)
+    rows_do("receive", 2)
+    col_do("receive", 2, whole, nb + 1)
 
     @pl.loop(0, nb)
     def _(b):
@@ -813,7 +827,7 @@
                     new = new + dinv[u, k, v] * rest[v]
                 out_a[k, u, here, :] = scale * new
 
-    for copy in (ds_copy, dv_copy, fp_copy, fs_low, fs_high):
+    for copy in (dv_copy, *upper, *lower):
         sent(copy)
     for n in range(2):
         incoming(n, 1 - odd, mine).wait_send()
@@ -831,13 +845,16 @@
         halo_face(0).wait_send()
         halo_face(1).wait_send()
 
-    halos_sent(0)
-    halos_sent(2)
+    rows_do("sent", 0)
+    rows_do("sent", 2)
+    col_do("sent", 0, whole, nb)
+    col_do("sent", 2, whole, nb + 1)
 
     @pl.loop(0, nb)
     def _(b):
         for kind in range(3):
             r_copy(kind, b, odd).wait_send()
+        col_do("sent", 1, pl.ds(pl.multiple_of(b * TILE, TILE), TILE), b)
 
 
 def finish(a, r, out_a, out_r, sems):
@@ -911,12 +928,12 @@
             dma((nb,)),
             dma((2,)),
             dma((2,)),
-            dma((3, 5)),
-            dma((3, 5)),
+            dma((3, 7)),
+            dma((3, 7)),
             dma((3, nb)),
             dma((3, nb)),
-            dma((3,)),
-            dma((3,)),
+            dma((nb + 2,)),
+            dma((nb + 2,)),
             dma((8,)),
             dma((8,)),
             dma((3,)),

time: 67.1 us -> 62 us (0.924)
  Pallas kernels: 64.6 us -> 59.5 us
    pallas_call x1, Pallas kernels: 62.9 us -> 57.9 us  [body(): pl.pallas_call(functools.partial(kernel, n_space, n_inst), out_shape=(pla...]
where the time goes in v5:
time: 62 us; the launch traced here: 61.5 us
  Pallas kernels  59.5 us (96%)
  between operations  1.93 us (3%)
    pallas_call x1, Pallas kernels, body(): pl.pallas_call(functools.partial(kernel, n_space, n_inst), out_shape=(pla...  57.9 us
    pallas_call x1, Pallas kernels, body(): pl.pallas_call(finish, out_shape=(out, out), in_specs=[vmem, vmem], out_s...  1.68 us

profile of v5, /device:TPU:0, one launch (start us, length us, event | category | flops | bytes accessed | tf_op | source)
XLA Modules:
  0.0 61.5 jit_solution(12696656190790853431)
XLA Ops:
  1.9 57.9 %shard_map.158 = (f32[2,6,64,512]{3,2,1,0:T(8,128)S(1)}, f32[2,6,64,512]{3,2,1,0:T(8,128)S(1)}) custom-call(f32[2,6,64,512]{3,2,1,0:T(8,128)} %a_hbm.1, f32[2,6,64,512]{3,2,1,0:T(8,128)} %s_hbm.1, f32[2,64,512]{2,1,0:T(8,128)} %fs_hbm.1, f32[2,64,512]{2,1,0:T(8,128)} %fp_hbm.1, f32[2,64,512]{2,1,0:T(8,128)} %ds_hbm.1, f32[64,512]{1,0:T(8,128)} %vol_hbm.1, ...), custom_call_target="tpu_custom_call" | custom-call | tf_op jit(solution)/shard_map/pallas_call | solution.py:887
  59.8 1.7 %shard_map.159 = (f32[2,6,64,512]{3,2,1,0:T(8,128)}, f32[2,6,64,512]{3,2,1,0:T(8,128)}) custom-call(f32[2,6,64,512]{3,2,1,0:T(8,128)S(1)} %get-tuple-element.4.a, f32[2,6,64,512]{3,2,1,0:T(8,128)S(1)} %get-tuple-element.5.r), custom_call_target="tpu_custom_call" | custom-call | tf_op jit(solution)/shard_map/pallas_call | solution.py:949

commit v6 on v5

--- a/solution.py
+++ b/solution.py
@@ -177,15 +177,15 @@
             semaphore, inc=1, device_id={"space": device}, device_id_type=MESH
         )
 
-    greet(barrier, partner)
+    even = me % 2 == 0
+
+    @pl.when(even)
+    def _():
+        greet(barrier, partner)
 
     @pl.when(has_hi)
     def _():
         greet(barrier, hi)
-
-    @pl.when(has_lo)
-    def _():
-        greet(barrier, lo)
 
     for copy in loads[:1] + tables + loads[1:]:
         copy.start()
@@ -225,7 +225,7 @@
 
     def dv_copy(kind, column, seat):
         return remote(
-            DV.at[0], DV.at[kind + 1], c_s.at[kind, 6], c_r.at[kind, 6], inst=peers[kind]
+            DV.at[0, pl.ds(0, 1)], DV.at[kind + 1, pl.ds(0, 1)], c_s.at[kind, 6], c_r.at[kind, 6], inst=peers[kind]
         )
 
     lower, upper = ([share(which, part) for which in range(3)] for part in range(2))
@@ -357,7 +357,7 @@
     lane8 = lax.broadcasted_iota(jnp.int32, (TILE, cols), 1)
     lane1 = lax.broadcasted_iota(jnp.int32, (TILE, LANES), 1)
 
-    pl.semaphore_wait(barrier, n_inst + has_hi.astype(jnp.int32) + has_lo.astype(jnp.int32))
+    pl.semaphore_wait(barrier, n_inst - 1 + has_lo.astype(jnp.int32) + me % 2)
 
     for copy in upper:
         start(copy, linked)
@@ -376,13 +376,13 @@
     DV[0] = packed
     start(dv_copy)
 
-    @pl.when(jnp.logical_not(has_hi))
-    def _():
-        greet(token.at[0], lo)
-
-    @pl.when(jnp.logical_not(has_lo))
-    def _():
-        greet(token.at[1], hi)
+    @pl.when(jnp.logical_not(even))
+    def _():
+        greet(token.at[2], partner)
+
+    @pl.when(has_lo)
+    def _():
+        greet(token.at[3], lo)
 
     sub_w = lax.broadcasted_iota(jnp.int32, (width, slots), 0)
     sub_h = lax.broadcasted_iota(jnp.int32, (cols, slots), 0)
@@ -461,21 +461,23 @@
     for copy in lower:
         start(copy, linked)
 
+    @pl.when(even)
+    def _():
+        pl.semaphore_wait(token.at[2], 1)
+
     @pl.when(has_hi)
     def _():
+        pl.semaphore_wait(token.at[3], 1)
         pl.semaphore_wait(token.at[0], 1)
 
-        @pl.when(has_lo)
-        def _():
-            greet(token.at[0], lo)
-
     @pl.when(has_lo)
     def _():
+        greet(token.at[0], lo)
         pl.semaphore_wait(token.at[1], 1)
 
-        @pl.when(has_hi)
-        def _():
-            greet(token.at[1], hi)
+    @pl.when(has_hi)
+    def _():
+        greet(token.at[1], hi)
 
     for copy in loads[1:]:
         copy.wait()
@@ -522,7 +524,7 @@
             kind = jnp.where(odd == position // per_dev, 0, 3)
         else:
             kind = jnp.where(odd == (position - CHIP) // per_dev, 1, 2)
-        vector = DV[kind]
+        vector = DV[kind, 0:1, :]
         for n in range(variables * variables):
             lane = (position % per_dev) * variables * variables + n
             DT[position * variables * variables + n] = jnp.broadcast_to(
@@ -940,7 +942,7 @@
             dma((3,)),
             dma((n_space,)),
             dma((n_space,)),
-            pltpu.SemaphoreType.REGULAR((2,)),
+            pltpu.SemaphoreType.REGULAR((4,)),
         ],
         compiler_params=pltpu.CompilerParams(
             collective_id=0, has_side_effects=True, vmem_limit_bytes=56 * 1024 * 1024

time: 62 us -> 61.5 us (level)
  no operation moved by 1% of the time
where the time goes in v6:
time: 61.5 us; the launch traced here: 61.4 us
  Pallas kernels  59.4 us (97%)
  between operations  1.93 us (3%)
    pallas_call x1, Pallas kernels, body(): pl.pallas_call(functools.partial(kernel, n_space, n_inst), out_shape=(pla...  57.8 us
    pallas_call x1, Pallas kernels, body(): pl.pallas_call(finish, out_shape=(out, out), in_specs=[vmem, vmem], out_s...  1.68 us

profile of v6, /device:TPU:0, one launch (start us, length us, event | category | flops | bytes accessed | tf_op | source)
XLA Modules:
  0.0 61.4 jit_solution(1639720360179949701)
XLA Ops:
  1.9 57.8 %shard_map.158 = (f32[2,6,64,512]{3,2,1,0:T(8,128)S(1)}, f32[2,6,64,512]{3,2,1,0:T(8,128)S(1)}) custom-call(f32[2,6,64,512]{3,2,1,0:T(8,128)} %a_hbm.1, f32[2,6,64,512]{3,2,1,0:T(8,128)} %s_hbm.1, f32[2,64,512]{2,1,0:T(8,128)} %fs_hbm.1, f32[2,64,512]{2,1,0:T(8,128)} %fp_hbm.1, f32[2,64,512]{2,1,0:T(8,128)} %ds_hbm.1, f32[64,512]{1,0:T(8,128)} %vol_hbm.1, ...), custom_call_target="tpu_custom_call" | custom-call | tf_op jit(solution)/shard_map/pallas_call | solution.py:889
  59.7 1.7 %shard_map.159 = (f32[2,6,64,512]{3,2,1,0:T(8,128)}, f32[2,6,64,512]{3,2,1,0:T(8,128)}) custom-call(f32[2,6,64,512]{3,2,1,0:T(8,128)S(1)} %get-tuple-element.4.a, f32[2,6,64,512]{3,2,1,0:T(8,128)S(1)} %get-tuple-element.5.r), custom_call_target="tpu_custom_call" | custom-call | tf_op jit(solution)/shard_map/pallas_call | solution.py:951

commit v7 on v6

--- a/solution.py
+++ b/solution.py
@@ -187,9 +187,6 @@
     def _():
         greet(barrier, hi)
 
-    for copy in loads[:1] + tables + loads[1:]:
-        copy.start()
-
     def incoming(n, target, seat):
         if n == 0:
             src, dst = a_hbm, AT.at[pair(seat), :, inner, :]
@@ -334,25 +331,6 @@
     def zeros(*shape):
         return jnp.zeros(shape, jnp.float32)
 
-    @pl.when(me == 0)
-    def _():
-        FS[:, 0:TILE, :] = zeros(instances, TILE, cols)
-        AT[:, :, 0:TILE, :] = zeros(CHIP, variables, TILE, cols)
-        Y[:, :, 0:TILE, :] = zeros(instances, variables, TILE, cols)
-
-    @pl.when(me == n_space - 1)
-    def _():
-        AT[:, :, rows + TILE : rows + 2 * TILE, :] = zeros(CHIP, variables, TILE, cols)
-        Y[:, :, rows + TILE : rows + 2 * TILE, :] = zeros(instances, variables, TILE, cols)
-
-    @pl.when(odd == 0)
-    def _():
-        CL[...] = zeros(3, rows, LANES)
-
-    @pl.when(odd == 1)
-    def _():
-        CR[...] = zeros(3, rows, LANES)
-
     sub8 = lax.broadcasted_iota(jnp.int32, (TILE, cols), 0)
     lane8 = lax.broadcasted_iota(jnp.int32, (TILE, cols), 1)
     lane1 = lax.broadcasted_iota(jnp.int32, (TILE, LANES), 1)
@@ -365,6 +343,28 @@
     for copy in upper + lower:
         start(copy, beside)
     incoming(1, 1 - odd, mine).start()
+
+    for copy in loads[:1] + tables + loads[1:]:
+        copy.start()
+
+    @pl.when(me == 0)
+    def _():
+        FS[:, 0:TILE, :] = zeros(instances, TILE, cols)
+        AT[:, :, 0:TILE, :] = zeros(CHIP, variables, TILE, cols)
+        Y[:, :, 0:TILE, :] = zeros(instances, variables, TILE, cols)
+
+    @pl.when(me == n_space - 1)
+    def _():
+        AT[:, :, rows + TILE : rows + 2 * TILE, :] = zeros(CHIP, variables, TILE, cols)
+        Y[:, :, rows + TILE : rows + 2 * TILE, :] = zeros(instances, variables, TILE, cols)
+
+    @pl.when(odd == 0)
+    def _():
+        CL[...] = zeros(3, rows, LANES)
+
+    @pl.when(odd == 1)
+    def _():
+        CR[...] = zeros(3, rows, LANES)
 
     tables[0].wait()
     packed = zeros(TILE, LANES)

time: 61.5 us -> 61.7 us (level)
  no operation moved by 1% of the time
where the time goes in v7:
time: 61.7 us; the launch traced here: 61.5 us
  Pallas kernels  59.6 us (97%)
  between operations  1.93 us (3%)
    pallas_call x1, Pallas kernels, body(): pl.pallas_call(functools.partial(kernel, n_space, n_inst), out_shape=(pla...  57.9 us
    pallas_call x1, Pallas kernels, body(): pl.pallas_call(finish, out_shape=(out, out), in_specs=[vmem, vmem], out_s...  1.68 us

profile of v7, /device:TPU:0, one launch (start us, length us, event | category | flops | bytes accessed | tf_op | source)
XLA Modules:
  0.0 61.5 jit_solution(17336408478679108954)
XLA Ops:
  1.9 57.9 %shard_map.158 = (f32[2,6,64,512]{3,2,1,0:T(8,128)S(1)}, f32[2,6,64,512]{3,2,1,0:T(8,128)S(1)}) custom-call(f32[2,6,64,512]{3,2,1,0:T(8,128)} %a_hbm.1, f32[2,6,64,512]{3,2,1,0:T(8,128)} %s_hbm.1, f32[2,64,512]{2,1,0:T(8,128)} %fs_hbm.1, f32[2,64,512]{2,1,0:T(8,128)} %fp_hbm.1, f32[2,64,512]{2,1,0:T(8,128)} %ds_hbm.1, f32[64,512]{1,0:T(8,128)} %vol_hbm.1, ...), custom_call_target="tpu_custom_call" | custom-call | tf_op jit(solution)/shard_map/pallas_call | solution.py:889
  59.8 1.7 %shard_map.159 = (f32[2,6,64,512]{3,2,1,0:T(8,128)}, f32[2,6,64,512]{3,2,1,0:T(8,128)}) custom-call(f32[2,6,64,512]{3,2,1,0:T(8,128)S(1)} %get-tuple-element.4.a, f32[2,6,64,512]{3,2,1,0:T(8,128)S(1)} %get-tuple-element.5.r), custom_call_target="tpu_custom_call" | custom-call | tf_op jit(solution)/shard_map/pallas_call | solution.py:951
